TPU v7x, 128 devices: a whole 4x4x4 slice. The times are simulated.
128 devices in a mesh: section: 16 (over x_hi, y, core), expert: 8 (over z, x_lo).
Axes of the slice: x: 4 (x_hi: 2, x_lo: 2; x = x_hi * 2 + x_lo), y: 4, z: 4, core: 2. Of those that a mesh axis runs over, the one named last changes fastest.
Arguments:
- fwd_input: bfloat16 [16, 1024, 2560], P('section', 'expert'), may hold values from -6 to 6
- back_input: bfloat16 [16, 1024, 2560], P('section', 'expert'), may hold values from -6 to 6
- cot_input: bfloat16 [16, 1024, 2560], P('section', 'expert'), may hold values from -6 to 6
- fwd_routes: int32 [16, 1024, 2], P('section', 'expert'), may hold values from 0 to 7, all different within a row; in each aligned block of 128 rows (0 to 127, 128 to 255, ..., all dimensions but the last counted through in order) at most 64 rows name the same one
- back_routes: int32 [16, 1024, 2], P('section', 'expert'), may hold values from 0 to 7, all different within a row; in each aligned block of 128 rows (0 to 127, 128 to 255, ..., all dimensions but the last counted through in order) at most 64 rows name the same one
- fwd_gates: float32 [16, 1024, 2], P('section', 'expert'), may hold values from 0.05 to 1
- back_gates: float32 [16, 1024, 2], P('section', 'expert'), may hold values from 0.05 to 1
- w_gate: bfloat16 [16, 8, 2560, 768], P('section', 'expert'), may hold values from -0.125 to 0.125
- w_up: bfloat16 [16, 8, 2560, 768], P('section', 'expert'), may hold values from -0.125 to 0.125
- w_down: bfloat16 [16, 8, 768, 2560], P('section', 'expert'), may hold values from -0.21875 to 0.21875
- norm_gain: float32 [16, 2560], P('section'), may hold values from 0.1 to 1.9
- verdict_head: float32 [2560], replicated, may hold values from -0.125 to 0.125
- verdict_labels: int32 [1024], P('expert'), may hold values from 0 to 1
Outputs:
- next_input: bfloat16 [16, 1024, 2560], P('section', 'expert')
- prev_grad: bfloat16 [16, 1024, 2560], P('section', 'expert')
- gain_grad: float32 [16, 2560], P('section')
- grad_gate: bfloat16 [16, 8, 2560, 768], P('section', 'expert')
- grad_up: bfloat16 [16, 8, 2560, 768], P('section', 'expert')
- grad_down: bfloat16 [16, 8, 768, 2560], P('section', 'expert')
Inputs may be any that keep to these rules, and one draw needn't show every extreme that they name: `fwd_routes`: each row names 2 different experts; within the rows of one device no expert is named by more than 64 rows, a bound that some block reaches. `back_routes`: as for fwd_routes.
All inputs are finite; a program needn't handle non-finite values.
Results may differ from a plain program's by a relative error of at most 0.012.
Values may be sent and summed in bfloat16 or wider, within the bound.
No kernel may reach another device: no remote copies, remote signals or barrier semaphores. Data moves between devices by JAX's collectives and lax.ppermute only.
A program may use at most 128 MiB of HBM per device.

v0:
```python
import functools
import math

import jax
import jax.numpy as jnp
from jax import lax
from jax.experimental import pallas as pl
from jax.experimental.pallas import tpu as pltpu
from jax.sharding import PartitionSpec as P

loss_scale = 64.0
norm_eps = 1e-06
bf16 = jnp.bfloat16
f32 = jnp.float32
chunk = 512
extra = 128
steps = (0, -1, 1, 2)
vmem = pl.BlockSpec(memory_space=pltpu.VMEM)
smem = pl.BlockSpec(memory_space=pltpu.SMEM)
anywhere = pl.BlockSpec(memory_space=pl.ANY)


def passed_along(value, axis, steps):
    count = lax.axis_size(axis)
    initial, last = (max(0, -steps), min(count, count - steps))
    return lax.ppermute(value, axis, [(source, source + steps) for source in range(initial, last)])


def slot_keys(ids, groups, capacity):
    tokens = ids.shape[0]
    lanes = lax.broadcasted_iota(jnp.int32, (tokens, 128), 1)
    hit0 = ids[:, 0:1] == lanes
    hit1 = ids[:, 1:2] == lanes
    hits = (hit0 | hit1).astype(bf16)
    before = (
        lax.broadcasted_iota(jnp.int32, (tokens, tokens), 1)
        < lax.broadcasted_iota(jnp.int32, (tokens, tokens), 0)
    ).astype(bf16)
    ranks = jnp.dot(before, hits, preferred_element_type=f32)
    rank0 = jnp.sum(jnp.where(hit0, ranks, 0.0), axis=1, keepdims=True).astype(jnp.int32)
    rank1 = jnp.sum(jnp.where(hit1, ranks, 0.0), axis=1, keepdims=True).astype(jnp.int32)
    return ids[:, 0:1] * capacity + rank0, ids[:, 1:2] * capacity + rank1


def slot_hits(ids, groups, capacity):
    key0, key1 = slot_keys(ids, groups, capacity)
    slots = lax.broadcasted_iota(jnp.int32, (ids.shape[0], groups * capacity), 1)
    return key0 == slots, key1 == slots


def split_weights(hit0, hit1, gates):
    weights = jnp.where(hit0, gates[:, 0:1], 0.0) + jnp.where(hit1, gates[:, 1:2], 0.0)
    high = weights.astype(bf16)
    low = (weights - high.astype(f32)).astype(bf16)
    return high, low


def over_tokens(left, right):
    return lax.dot_general(left, right, (((0,), (0,)), ((), ())), preferred_element_type=f32)


def over_chunks(width, body, carry=None):
    for at in range(0, width, chunk):
        carry = body(slice(at, at + chunk), carry)
    return carry


def loop_chunks(width, body, carry):
    def step(at, carry):
        return body(pl.ds(pl.multiple_of(at * chunk, chunk), chunk), carry)

    return lax.fori_loop(0, width // chunk, step, carry)


def columns(table):
    return table.T


def as_ids(pair):
    return pair.astype(jnp.int32)


def ranked(hit):
    tokens = hit.shape[0]
    before = (
        lax.broadcasted_iota(jnp.int32, (tokens, tokens), 1)
        < lax.broadcasted_iota(jnp.int32, (tokens, tokens), 0)
    ).astype(bf16)
    return jnp.dot(before, hit.astype(bf16), preferred_element_type=f32).astype(jnp.int32)


def pick_rows(
    field,
    groups,
    capacity,
    place_ref,
    table_ref,
    own_ref,
    below_ref,
    above_ref,
    far_low_ref,
    far_high_ref,
    gain_ref,
    near_ref,
    other_ref,
):
    mine = place_ref[1]
    tokens, width = own_ref.shape
    lanes = lax.broadcasted_iota(jnp.int32, (tokens, 2 * capacity), 1)
    wanted = jnp.where(lanes < capacity, mine, mine ^ 1)

    def far(cols):
        return jnp.concatenate([far_low_ref[:, cols], far_high_ref[:, cols]], axis=0)

    readers = (
        lambda cols: own_ref[:, cols],
        lambda cols: below_ref[:, cols],
        lambda cols: above_ref[:, cols],
        far,
    )
    picks = []
    for source in sources(mine)[:4]:
        ids = as_ids(columns(table_ref[source])[:, field : field + 2])
        hit = (ids[:, 0:1] == wanted) | (ids[:, 1:2] == wanted)
        picks.append((hit & (ranked(hit) == (lanes & (capacity - 1)))).astype(bf16))

    def square(cols, totals):
        rows = [read(cols).astype(f32) for read in readers]
        return tuple(
            total + jnp.sum(x * x, axis=1, keepdims=True) for total, x in zip(totals, rows)
        )

    totals = loop_chunks(width, square, (jnp.zeros((tokens, 1), f32),) * 4)
    invs = [lax.rsqrt(total / width + norm_eps) for total in totals]

    def fill(cols, carry):
        for at, read in enumerate(readers):
            normed = (read(cols).astype(f32) * invs[at] * gain_ref[:, cols]).astype(bf16)
            got = over_tokens(picks[at], normed).astype(bf16)
            place = slice(at * capacity, (at + 1) * capacity)
            near_ref[place, cols] = got[:capacity]
            other_ref[place, cols] = got[capacity:]
        return carry

    loop_chunks(width, fill, 0)


def weigh_rows(groups, capacity, place_ref, table_ref, own_ref, pair_ref, head_ref, *out_refs):
    is_last = place_ref[0] == 1
    mine = place_ref[1]
    tokens, width = own_ref.shape
    lanes = lax.broadcasted_iota(jnp.int32, (tokens, len(out_refs) * capacity), 1)
    wanted = (mine + 2 * lax.div(lanes, capacity)) & (groups - 1)
    weights = []
    for side in range(2):
        fields = columns(table_ref[mine ^ side])
        ids = as_ids(fields[:, 2:4])
        hit0, hit1 = ids[:, 0:1] == wanted, ids[:, 1:2] == wanted
        inside = ranked(hit0 | hit1) == (lanes & (capacity - 1))
        weights.append(split_weights(hit0 & inside, hit1 & inside, fields[:, 4:6]))

    def fill(cols, carry):
        for side, cot_ref in enumerate((own_ref, pair_ref)):
            high, low = weights[side]
            cot = cot_ref[:, cols]
            head = jnp.broadcast_to(head_ref[:, cols], cot.shape)
            head_high = head.astype(bf16)
            head_low = (head - head_high.astype(f32)).astype(bf16)
            cot_high = jnp.where(is_last, head_high.astype(f32), cot.astype(f32)).astype(bf16)
            cot_low = jnp.where(is_last, head_low.astype(f32), 0.0).astype(bf16)
            dout = (
                over_tokens(high, cot_high) + over_tokens(low, cot_high) + over_tokens(high, cot_low)
            ).astype(bf16)
            for at, ref in enumerate(out_refs):
                ref[side * capacity : (side + 1) * capacity, cols] = dout[
                    at * capacity : (at + 1) * capacity
                ]
        return carry

    loop_chunks(width, fill, 0)


def in_parts(column):
    lanes = lax.broadcasted_iota(jnp.int32, (column.shape[0], extra), 1)
    out = jnp.zeros((column.shape[0], extra), f32)
    rest = column
    for lane in range(3):
        part = rest.astype(bf16).astype(f32)
        out = jnp.where(lanes == lane, part, out)
        rest = rest - part
    return out.astype(bf16)


def sources(mine):
    return [((mine + 2 * (step + 4)) & 7) ^ side for side in (0, 1) for step in steps]


def attach_dots(groups, capacity, place_ref, out_ref, head_ref, ret_ref, dots_ref):
    width = out_ref.shape[1]
    rows = lax.broadcasted_iota(jnp.int32, (8, width), 0)
    parts = jnp.zeros((8, width), f32)
    rest = head_ref[...]
    for row in range(3):
        part = rest.astype(bf16).astype(f32)
        parts = jnp.where(rows == row, part, parts)
        rest = rest - part
    parts = parts.astype(bf16)
    for at, source in enumerate(sources(place_ref[1])):
        out = out_ref[at * capacity : (at + 1) * capacity, :]
        ret_ref[source, :, :width] = out
        ret_ref[source, :, width:] = jnp.zeros((capacity, extra), bf16)
        dots = lax.dot_general(parts, out, (((1,), (1,)), ((), ())), preferred_element_type=f32)
        dots_ref[source] = jnp.sum(dots, axis=0, keepdims=True)


def split_rows(groups, capacity, place_ref, in_ref, out_ref):
    for at, source in enumerate(sources(place_ref[1])):
        out_ref[source] = in_ref[at * capacity : (at + 1) * capacity, :]


def find_coefs(
    groups,
    capacity,
    place_ref,
    table_ref,
    x_ref,
    head_ref,
    labels_ref,
    dots_ref,
    unused_ref,
    coef_ref,
    block_ref,
):
    is_last = place_ref[0] == 1
    fields = columns(table_ref[...])
    hit0, hit1 = slot_hits(as_ids(fields[:, 0:2]), groups, capacity)
    pick = (hit0 | hit1).astype(bf16)
    weights = jnp.where(hit0, fields[:, 6:7], 0.0) + jnp.where(hit1, fields[:, 7:8], 0.0)

    def add(cols, logits):
        return logits + jnp.sum(
            x_ref[:, cols].astype(f32) * head_ref[:, cols], axis=1, keepdims=True
        )

    logits = over_chunks(x_ref.shape[1], add, jnp.zeros((x_ref.shape[0], 1), f32))
    for at in range(groups):
        block = weights[:, at * capacity : (at + 1) * capacity]
        logits += jnp.sum(block * dots_ref[at], axis=1, keepdims=True)
    coef = loss_scale * (jax.nn.sigmoid(logits) - labels_ref[...].astype(f32))
    coef = jnp.where(is_last, coef, 1.0)
    coef_ref[...] = coef
    picked = over_tokens(pick, in_parts(coef))
    ones = (lax.broadcasted_iota(jnp.int32, picked.shape, 1) == 0).astype(f32)
    block_ref[...] = jnp.where(is_last, picked, ones).astype(bf16)


def join_forward(groups, capacity, table_ref, ret_ref, x_ref, out_ref):
    fields = columns(table_ref[...])
    hit0, hit1 = slot_hits(as_ids(fields[:, 0:2]), groups, capacity)
    high, low = split_weights(hit0, hit1, fields[:, 6:8])

    def fill(cols, carry):
        ret = ret_ref[:, cols]
        mixed = jnp.dot(high, ret, preferred_element_type=f32) + jnp.dot(
            low, ret, preferred_element_type=f32
        )
        out_ref[:, cols] = (x_ref[:, cols].astype(f32) + mixed).astype(bf16)
        return carry

    loop_chunks(x_ref.shape[1], fill, 0)


def copy_rows(in_ref, unused_ref, out_ref):
    out_ref[...] = in_ref[...]


def assemble(pieces, *refs):
    sources_refs, out_ref, sems = refs[:-2], refs[-2], refs[-1]
    copies = []
    for at, (which, start, rows, to) in enumerate(pieces):
        copy = pltpu.make_async_copy(
            sources_refs[which].at[pl.ds(start, rows)], out_ref.at[pl.ds(to, rows)], sems.at[at]
        )
        copy.start()
        copies.append(copy)
    for copy in copies:
        copy.wait()


def join_backward(
    groups,
    capacity,
    place_ref,
    table_ref,
    ret_ref,
    x_ref,
    cot_ref,
    coef_ref,
    gain_ref,
    head_ref,
    out_ref,
    grad_ref,
    normed_ref,
):
    is_last = place_ref[0] == 1
    fields = columns(table_ref[...])
    hit0, hit1 = slot_hits(as_ids(fields[:, 2:4]), groups, capacity)
    pick = (hit0 | hit1).astype(bf16)
    coef = coef_ref[...]
    tokens, width = x_ref.shape
    zero = jnp.zeros((tokens, 1), f32)

    def square(cols, total):
        x = x_ref[:, cols].astype(f32)
        return total + jnp.sum(x * x, axis=1, keepdims=True)

    inv = lax.rsqrt(over_chunks(width, square, zero) / width + norm_eps)

    def first(cols, dots):
        d_normed = coef * jnp.dot(pick, ret_ref[:, cols], preferred_element_type=f32)
        normed_ref[:, cols] = d_normed
        product = d_normed * x_ref[:, cols].astype(f32)
        grad_ref[:, cols] = jnp.sum(product * inv, axis=0, keepdims=True)
        return dots + jnp.sum(product * gain_ref[:, cols], axis=1, keepdims=True)

    scale = inv * inv * inv * (over_chunks(width, first, zero) / width)

    def second(cols, carry):
        cot = jnp.where(is_last, coef * head_ref[:, cols], cot_ref[:, cols].astype(f32))
        out_ref[:, cols] = (
            cot
            + inv * (gain_ref[:, cols] * normed_ref[:, cols])
            - x_ref[:, cols].astype(f32) * scale
        ).astype(bf16)
        return carry

    over_chunks(width, second, 0)


def call(kernel, name, outs, args, specs, scratch=(), out_specs=None, aliases=None, flops=0):
    moved = sum(value.size * value.dtype.itemsize for value in args)
    moved += sum(math.prod(shape) * jnp.dtype(dtype).itemsize for shape, dtype in outs)
    return pl.pallas_call(
        kernel,
        cost_estimate=pl.CostEstimate(flops=flops, transcendentals=0, bytes_accessed=moved),
        out_shape=[jax.ShapeDtypeStruct(shape, dtype) for shape, dtype in outs],
        grid=(1,),
        in_specs=specs,
        out_specs=out_specs or [vmem] * len(outs),
        scratch_shapes=list(scratch),
        input_output_aliases=aliases or {},
        compiler_params=pltpu.CompilerParams(vmem_limit_bytes=48 << 20),
        name=name,
    )(*args)


def contract_rows(left_op, right_op):
    return lax.dot_general(
        left_op, right_op, (((0,), (0,)), ((), ())), preferred_element_type=f32
    )


def contract_cols(left_op, right_op):
    return lax.dot_general(
        left_op, right_op, (((1,), (1,)), ((), ())), preferred_element_type=f32
    )


def on_device(
    fwd_input,
    back_input,
    cot_input,
    fwd_routes,
    back_routes,
    fwd_gates,
    back_gates,
    w_gate,
    w_up,
    w_down,
    norm_gain,
    verdict_head,
    verdict_labels,
):
    sections = lax.axis_size("section")
    groups = lax.axis_size("expert")
    tok_dev, width = fwd_input.shape[1:]
    top_k = fwd_routes.shape[2]
    capacity = min(tok_dev, 2 * tok_dev * top_k // groups)
    slots = groups * capacity
    x_fwd, x_back, cot = fwd_input[0], back_input[0], cot_input[0]
    wg, wu, wd = w_gate[0, 0], w_up[0, 0], w_down[0, 0]
    head = verdict_head[None]

    def bind(kernel):
        def bound(*refs):
            kernel(groups, capacity, *refs)

        return bound

    def exchange(value):
        return lax.all_to_all(value, "expert", split_axis=0, concat_axis=0, tiled=True)

    def move(value, dz, dx):
        return lax.ppermute(
            value,
            "expert",
            [
                (source, ((source + 2 * dz) % groups) ^ dx)
                for source in range(groups)
            ],
        )

    half = tok_dev // 2

    def along_z(value):
        below, above = move(value, 1, 0), move(value, -1, 0)
        return below, above

    def far_along_z(below, above):
        return move(below[:half], 1, 0), move(above[half:], -1, 0)

    mine = lax.axis_index("expert")
    is_last = lax.axis_index("section") == sections - 1
    place = jnp.stack([is_last.astype(jnp.int32), mine])
    below_f, above_f = along_z(x_fwd)
    pair_cot = move(cot, 0, 1)
    below_f, above_f, pair_cot = lax.optimization_barrier((below_f, above_f, pair_cot))
    x_sel = jnp.where(is_last, x_fwd, x_back)
    table = jnp.concatenate(
        [
            fwd_routes[0].T.astype(f32),
            jnp.where(is_last, fwd_routes[0], back_routes[0]).T.astype(f32),
            jnp.where(is_last, fwd_gates[0], back_gates[0]).T,
            fwd_gates[0].T,
        ],
        axis=0,
    )
    tables = exchange(jnp.broadcast_to(table[None], (groups,) + table.shape))
    order = jnp.stack(sources(mine))

    def picked(field, own, below, above, far):
        return call(
            functools.partial(pick_rows, field, groups, capacity),
            "pick_rows",
            [((slots // 2, width), bf16)] * 2,
            (place, tables, own, below, above, *far, norm_gain),
            [smem] + [vmem] * 7,
            flops=4 * slots * tok_dev * width,
        )

    def assembled(blocks, pieces):
        return call(
            functools.partial(assemble, pieces),
            "assemble",
            [((slots, width), bf16)],
            blocks,
            [anywhere] * len(blocks),
            [pltpu.SemaphoreType.DMA((len(pieces),))],
            out_specs=[anywhere],
        )[0]

    far_f = far_along_z(below_f, above_f)
    tables, far_f = lax.optimization_barrier((tables, far_f))
    below_f, above_f, x_ring = lax.optimization_barrier((below_f, above_f, x_sel))
    below_b, above_b = along_z(x_ring)
    near_f, other_f = picked(0, x_fwd, below_f, above_f, far_f)
    other_f = move(other_f, 0, 1)
    send_d = call(
        bind(weigh_rows),
        "weigh_rows",
        [((2 * capacity, width), bf16)] * 4,
        (place, tables, cot, pair_cot, head),
        [smem] + [vmem] * 4,
        flops=8 * slots * tok_dev * width,
    )
    below_b, above_b, send_d = lax.optimization_barrier((below_b, above_b, send_d))
    far_b = far_along_z(below_b, above_b)
    near_b, other_b = picked(2, x_sel, below_b, above_b, far_b)
    other_b, send_d = lax.optimization_barrier((other_b, send_d))
    other_b = move(other_b, 0, 1)
    got_d = [move(send_d[step % 4], step, 0) if step else send_d[0] for step in (0, 1, 3, 2)]

    halves = [(0, 0, slots // 2, 0), (1, 0, slots // 2, slots // 2)]
    quarters = [
        (at, side * capacity, capacity, (side * 4 + at) * capacity)
        for side in range(2)
        for at in range(4)
    ]
    rows_f = assembled((near_f, other_f), halves)
    gate_pre = jnp.dot(rows_f, wg, preferred_element_type=f32)
    up_pre = jnp.dot(rows_f, wu, preferred_element_type=f32)
    hidden_f = lax.optimization_barrier((jax.nn.silu(gate_pre) * up_pre).astype(bf16))
    out_f = jnp.dot(hidden_f, wd, preferred_element_type=f32).astype(bf16)
    ret_send, dots = call(
        bind(attach_dots),
        "attach_dots",
        [((groups, capacity, width + extra), bf16), ((groups, 1, capacity), f32)],
        (place, out_f, head),
        [smem, vmem, vmem],
    )
    dots = exchange(dots)
    last_block = pl.BlockSpec((slots, extra), lambda i: (0, width // extra))
    coef, ret_send = call(
        bind(find_coefs),
        "find_coefs",
        [((tok_dev, 1), f32), ((slots, width + extra), bf16)],
        (
            place,
            table,
            x_fwd,
            head,
            verdict_labels[:, None],
            dots,
            ret_send.reshape(slots, width + extra),
        ),
        [smem] + [vmem] * 5 + [last_block],
        out_specs=[vmem, last_block],
        aliases={6: 1},
    )
    got_d, other_b, ret_send = lax.optimization_barrier((got_d, other_b, ret_send))
    ret_f = exchange(ret_send.reshape(groups, capacity, width + extra))
    ret_f = ret_f.reshape(slots, width + extra)
    rows_b = assembled((near_b, other_b), halves)
    rows_d = assembled(tuple(got_d), quarters)

    gate_pre = jnp.dot(rows_b, wg, preferred_element_type=f32)
    up_pre = jnp.dot(rows_b, wu, preferred_element_type=f32)
    sig = jax.nn.sigmoid(gate_pre)
    silu = gate_pre * sig
    hidden_b = (silu * up_pre).astype(bf16)
    d_hidden = contract_cols(rows_d, wd)
    d_gate = (d_hidden * up_pre * sig * (1.0 + gate_pre * (1.0 - sig))).astype(bf16)
    d_up = (d_hidden * silu).astype(bf16)
    d_rows = (contract_cols(d_gate, wg) + contract_cols(d_up, wu)).astype(bf16)

    (d_rows,) = call(
        bind(split_rows),
        "split_rows",
        [((groups, capacity, width), bf16)],
        (place, d_rows),
        [smem, vmem],
    )
    ret_f, d_rows = lax.optimization_barrier((ret_f, d_rows))
    ret_d = exchange(d_rows).reshape(slots, width)
    (layer_out,) = call(
        bind(join_forward),
        "join_forward",
        [((tok_dev, width), bf16)],
        (table, ret_f, x_fwd),
        [vmem] * 3,
    )
    next_input = passed_along(layer_out, "section", 1)
    coef_rows = jnp.sum(ret_f[:, width:].astype(f32), axis=1).reshape(groups, capacity)
    coef_rows = jnp.take(coef_rows, order, axis=0).reshape(slots, 1)

    def scaled(value):
        return (value.astype(f32) * coef_rows).astype(bf16)

    grad_d = contract_rows(scaled(hidden_b), rows_d).astype(bf16)
    grad_g = contract_rows(rows_b, scaled(d_gate)).astype(bf16)
    grad_u = contract_rows(rows_b, scaled(d_up)).astype(bf16)

    ret_d, grad_d, grad_g, grad_u = lax.optimization_barrier((ret_d, grad_d, grad_g, grad_u))
    d_input, gain_local = call(
        bind(join_backward),
        "join_backward",
        [((tok_dev, width), bf16), ((1, width), f32)],
        (place, table, ret_d, x_sel, cot, coef, norm_gain, head),
        [smem] + [vmem] * 7,
        [pltpu.VMEM((tok_dev, width), f32)],
    )
    prev_grad = passed_along(d_input, "section", -1)
    (next_input,) = call(
        copy_rows, "copy_rows", [((tok_dev, width), bf16)], (next_input, gain_local), [vmem] * 2
    )
    gain_grad = gain_local
    step = 1
    while step < groups:
        gain_grad = gain_grad + lax.ppermute(
            gain_grad, "expert", [(source, source ^ step) for source in range(groups)]
        )
        step *= 2
    return (
        next_input[None],
        prev_grad[None],
        gain_grad,
        grad_g[None, None],
        grad_u[None, None],
        grad_d[None, None],
    )


def solution(mesh):
    return jax.shard_map(
        on_device,
        mesh=mesh,
        in_specs=(
            P("section", "expert", None),
            P("section", "expert", None),
            P("section", "expert", None),
            P("section", "expert", None),
            P("section", "expert", None),
            P("section", "expert", None),
            P("section", "expert", None),
            P("section", "expert", None, None),
            P("section", "expert", None, None),
            P("section", "expert", None, None),
            P("section", None),
            P(),
            P("expert"),
        ),
        out_specs=(
            P("section", "expert", None),
            P("section", "expert", None),
            P("section", None),
            P("section", "expert", None, None),
            P("section", "expert", None, None),
            P("section", "expert", None, None),
        ),
        check_vma=False,
    )
```

profile of v0, /device:TPU:4, one launch (start us, length us, event | category | flops | bytes accessed | tf_op | source)
XLA Modules:
  0.0 194.7 jit_solution(3434213716010145813)
XLA Ops:
  0.7 2.0 %collective-permute-start = (bf16[128,2560]{1,0:T(8,128)(2,1)}, bf16[128,2560]{1,0:T(8,128)(2,1)S(1)}, u32[]{:S(2)}, u32[]{:S(2)}) collective-permute-start(bf16[128,2560]{1,0:T(8,128)(2,1)} %bitcast.91), channel_id=1, source_target_pairs={{0,2},{1,3},{2,4},{3,5},{4,6},{5,7},{6,0},{7,1},{8,10},{9,11},{10,... | collective-permute-start | bytes 1966088 | tf_op jit(solution)/shard_map/ppermute | solution.py:404
  2.6 2.2 %collective-permute-start.1 = (bf16[128,2560]{1,0:T(8,128)(2,1)}, bf16[128,2560]{1,0:T(8,128)(2,1)S(1)}, u32[]{:S(2)}, u32[]{:S(2)}) collective-permute-start(bf16[128,2560]{1,0:T(8,128)(2,1)} %bitcast.92), channel_id=1, source_target_pairs={{0,6},{1,7},{2,0},{3,1},{4,2},{5,3},{6,4},{7,5},{8,14},{9,15},{10,... | collective-permute-start | bytes 1966088 | tf_op jit(solution)/shard_map/ppermute | solution.py:404
  4.8 1.2 collective-permute-start.2
  8.8 3.5 %all-to-all-start = ((f32[8,8,128]{2,1,0:T(8,128)}), f32[8,8,128]{2,1,0:T(8,128)S(1)}, u32[]{:S(2)}, u32[]{:S(2)}) async-start(f32[8,8,128]{2,1,0:T(8,128)} %broadcast_in_dim.37), calls=%async_computation | async-start | bytes 65536 | tf_op jit(solution)/shard_map/all_to_all | solution.py:401
  12.3 7.5 %collective-permute-done.below_ref = bf16[128,2560]{1,0:T(8,128)(2,1)S(1)} collective-permute-done((bf16[128,2560]{1,0:T(8,128)(2,1)}, bf16[128,2560]{1,0:T(8,128)(2,1)S(1)}, u32[]{:S(2)}, u32[]{:S(2)}) %collective-permute-start) | collective-permute-done | bytes 655392 | tf_op jit(solution)/shard_map/ppermute | solution.py:404
  19.8 1.7 collective-permute-done.2.refs_3_
  23.0 3.2 %collective-permute-start.4 = (bf16[64,2560]{1,0:T(8,128)(2,1)}, bf16[64,2560]{1,0:T(8,128)(2,1)}, u32[]{:S(2)}, u32[]{:S(2)}) collective-permute-start(bf16[64,2560]{1,0:T(8,128)(2,1)} %slice.16), channel_id=1, source_target_pairs={{0,6},{1,7},{2,0},{3,1},{4,2},{5,3},{6,4},{7,5},{8,14},{9,15},{10,... | collective-permute-start | bytes 983048 | tf_op jit(solution)/shard_map/ppermute | solution.py:404
  26.2 1.4 bitcast_select_fusion.own_ref.refs_3_
  27.7 4.2 %collective-permute-done.3.far_low_ref = bf16[64,2560]{1,0:T(8,128)(2,1)} collective-permute-done((bf16[64,2560]{1,0:T(8,128)(2,1)}, bf16[64,2560]{1,0:T(8,128)(2,1)}, u32[]{:S(2)}, u32[]{:S(2)}) %collective-permute-start.3) | collective-permute-done | bytes 327712 | tf_op jit(solution)/shard_map/ppermute | solution.py:404
  31.8 5.3 %pick_rows.3 = (bf16[256,2560]{1,0:T(8,128)(2,1)S(1)}, bf16[256,2560]{1,0:T(8,128)(2,1)}) custom-call(s32[2]{0:T(128)S(1)} %pad_add_fusion.refs_0_.place_ref, f32[8,8,128]{2,1,0:T(8,128)S(1)} %all-to-all-done.refs_1_.table_ref, bf16[128,2560]{1,0:T(8,128)(2,1)S(1)} %bitcast.93, bf16[128,2560]{1,0:T(8,128)(2,1)S(1)} %collective-permute-done.below_ref, ...), custom_call_target="tpu_custom_call" | custom-call | flops 671088640 | bytes 5285896 | tf_op jit(solution)/shard_map/pick_rows/pallas_call | solution.py:343
  37.1 1.1 copy-done.9
  38.2 1.2 collective-permute-start.13
  40.1 2.9 %collective-permute-start.6 = (bf16[128,2560]{1,0:T(8,128)(2,1)S(1)}, bf16[128,2560]{1,0:T(8,128)(2,1)S(1)}, u32[]{:S(2)}, u32[]{:S(2)}) collective-permute-start(bf16[128,2560]{1,0:T(8,128)(2,1)S(1)} %bitcast_select_fusion.own_ref.refs_3_), channel_id=1, source_target_pairs={{0,6},{1,7},{2,0},{3,1},{4,2},{5,3},{6,4},{7,5},{8,14},{9,15},{10,... | collective-permute-start | bytes 1966088 | tf_op jit(solution)/shard_map/ppermute | solution.py:404
  43.1 5.2 %weigh_rows.1 = (bf16[128,2560]{1,0:T(8,128)(2,1)S(1)}, bf16[128,2560]{1,0:T(8,128)(2,1)}, bf16[128,2560]{1,0:T(8,128)(2,1)}, bf16[128,2560]{1,0:T(8,128)(2,1)}) custom-call(s32[2]{0:T(128)S(1)} %pad_add_fusion.refs_0_.place_ref, f32[8,8,128]{2,1,0:T(8,128)S(1)} %all-to-all-done.refs_1_.table_ref, bf16[128,2560]{1,0:T(8,128)(2,1)S(1)} %bitcast.97, ...), custom_call_target="tpu_custom_call" | custom-call | flops 1342177280 | bytes 3975176 | tf_op jit(solution)/shard_map/weigh_rows/pallas_call | solution.py:343
  48.3 0.8 copy-done.15
  49.1 5.8 %collective-permute-done.5.below_ref = bf16[128,2560]{1,0:T(8,128)(2,1)S(1)} collective-permute-done((bf16[128,2560]{1,0:T(8,128)(2,1)S(1)}, bf16[128,2560]{1,0:T(8,128)(2,1)S(1)}, u32[]{:S(2)}, u32[]{:S(2)}) %collective-permute-start.5) | collective-permute-done | bytes 655392 | tf_op jit(solution)/shard_map/ppermute | solution.py:404
  55.7 1.1 collective-permute-start.7
  57.6 2.1 %collective-permute-start.8 = (bf16[64,2560]{1,0:T(8,128)(2,1)}, bf16[64,2560]{1,0:T(8,128)(2,1)S(1)}, u32[]{:S(2)}, u32[]{:S(2)}) collective-permute-start(bf16[64,2560]{1,0:T(8,128)(2,1)} %slice.18), channel_id=1, source_target_pairs={{0,6},{1,7},{2,0},{3,1},{4,2},{5,3},{6,4},{7,5},{8,14},{9,15},{10,... | collective-permute-start | bytes 983048 | tf_op jit(solution)/shard_map/ppermute | solution.py:404
  59.8 4.4 %collective-permute-done.7.far_low_ref = bf16[64,2560]{1,0:T(8,128)(2,1)S(1)} collective-permute-done((bf16[64,2560]{1,0:T(8,128)(2,1)}, bf16[64,2560]{1,0:T(8,128)(2,1)S(1)}, u32[]{:S(2)}, u32[]{:S(2)}) %collective-permute-start.7) | collective-permute-done | bytes 327712 | tf_op jit(solution)/shard_map/ppermute | solution.py:404
  64.9 4.7 %pick_rows.2 = (bf16[256,2560]{1,0:T(8,128)(2,1)S(1)}, bf16[256,2560]{1,0:T(8,128)(2,1)}) custom-call(s32[2]{0:T(128)S(1)} %pad_add_fusion.refs_0_.place_ref, f32[8,8,128]{2,1,0:T(8,128)S(1)} %all-to-all-done.refs_1_.table_ref, bf16[128,2560]{1,0:T(8,128)(2,1)S(1)} %bitcast_select_fusion.own_ref.refs_3_, ...), custom_call_target="tpu_custom_call" | custom-call | flops 671088640 | bytes 5285896 | tf_op jit(solution)/shard_map/pick_rows/pallas_call | solution.py:343
  69.6 1.1 copy-done.11
  70.6 1.7 collective-permute-start.9
  72.4 1.6 collective-permute-start.10
  73.9 2.0 %collective-permute-start.11 = (bf16[128,2560]{1,0:T(8,128)(2,1)}, bf16[128,2560]{1,0:T(8,128)(2,1)}, u32[]{:S(2)}, u32[]{:S(2)}) collective-permute-start(bf16[128,2560]{1,0:T(8,128)(2,1)} %get-tuple-element.71), channel_id=1, source_target_pairs={{0,4},{1,5},{2,6},{3,7},{4,0},{5,1},{6,2},{7,3},{8,12},{9,13},{10,... | collective-permute-start | bytes 1966088 | tf_op jit(solution)/shard_map/ppermute | solution.py:404
  75.9 0.8 collective-permute-start.12
  76.8 1.6 assemble.3
  78.4 0.9 copy-done.26
  79.3 2.2 %fusion.12 = f32[512,768]{1,0:T(8,128)S(1)} fusion(bf16[512,2560]{1,0:T(8,128)(2,1)S(1)} %assemble.3, bf16[1,1,2560,768]{3,2,1,0:T(8,128)(2,1)S(1)} %copy-done.26), kind=kOutput, calls=%fused_computation.18 | convolution fusion | flops 2013265920 | bytes 8126464 | tf_op jit(solution)/shard_map/dot_general | solution.py:490
  81.5 2.3 %multiply_convert_fusion.6 = bf16[512,768]{1,0:T(8,128)(2,1)S(1)} fusion(f32[512,768]{1,0:T(8,128)S(1)} %fusion.12, bf16[512,2560]{1,0:T(8,128)(2,1)S(1)} %assemble.3, bf16[1,1,2560,768]{3,2,1,0:T(8,128)(2,1)S(1)} %copy-done.28), kind=kOutput, calls=%fused_computation.28 | convolution fusion | flops 2015625216 | bytes 8912896 | tf_op jit(solution)/shard_map/dot_general | solution.py:491
  83.8 2.2 %convolution_convert_fusion.3.refs_1_ = bf16[512,2560]{1,0:T(8,128)(2,1)S(1)} fusion(bf16[512,768]{1,0:T(8,128)(2,1)S(1)} %multiply_convert_fusion.6, bf16[1,1,768,2560]{3,2,1,0:T(8,128)(2,1)S(1)} %copy-done.24), kind=kOutput, calls=%fused_computation.5 | convolution fusion | flops 2014576640 | bytes 7340032 | tf_op jit(solution)/shard_map/dot_general | solution.py:493
  86.0 2.0 %attach_dots.1 = (bf16[8,64,2688]{2,1,0:T(8,128)(2,1)S(1)}, f32[8,1,64]{2,1,0:T(1,128)}) custom-call(s32[2]{0:T(128)S(1)} %pad_add_fusion.refs_0_.place_ref, bf16[512,2560]{1,0:T(8,128)(2,1)S(1)} %convolution_convert_fusion.3.refs_1_, f32[1,2560]{1,0:T(1,128)S(1)} %broadcast_in_dim.38.refs_4_.refs_2_.refs_3_.refs_7_), custom_call_target="tpu_custom_call" | custom-call | bytes 5386248 | tf_op jit(solution)/shard_map/attach_dots/pallas_call | solution.py:343
  88.0 3.4 %all-to-all-start.1 = ((f32[8,1,64]{2,1,0:T(1,128)}), f32[8,1,64]{2,1,0:T(1,128)S(1)}, u32[]{:S(2)}, u32[]{:S(2)}) async-start(f32[8,1,64]{2,1,0:T(1,128)} %get-tuple-element.79), calls=%async_computation.1 | async-start | bytes 8192 | tf_op jit(solution)/shard_map/all_to_all | solution.py:401
  91.6 10.5 %all-to-all-done.1.refs_5_ = f32[8,1,64]{2,1,0:T(1,128)S(1)} async-done(((f32[8,1,64]{2,1,0:T(1,128)}), f32[8,1,64]{2,1,0:T(1,128)S(1)}, u32[]{:S(2)}, u32[]{:S(2)}) %all-to-all-start.1) | async-done | bytes 2080 | tf_op jit(solution)/shard_map/all_to_all | solution.py:401
  102.2 2.0 %find_coefs.1 = (f32[128,1]{1,0:T(8,128)S(1)}, bf16[512,2688]{1,0:T(8,128)(2,1)S(1)}) custom-call(s32[2]{0:T(128)S(1)} %pad_add_fusion.refs_0_.place_ref, f32[8,128]{1,0:T(8,128)S(1)} %pad_maximum_fusion.refs_1_.refs_0_, bf16[128,2560]{1,0:T(8,128)(2,1)S(1)} %bitcast.94, ...), custom_call_target="tpu_custom_call", output_to_operand_aliasing={{1}: (6, {})} | custom-call | bytes 6177800 | tf_op jit(solution)/shard_map/find_coefs/pallas_call | solution.py:343
  104.2 1.5 copy-done
  106.3 3.9 %all-to-all-start.2 = ((bf16[8,64,2688]{2,1,0:T(8,128)(2,1)}), bf16[8,64,2688]{2,1,0:T(8,128)(2,1)S(1)}, u32[]{:S(2)}, u32[]{:S(2)}) async-start(bf16[8,64,2688]{2,1,0:T(8,128)(2,1)} %bitcast.90), calls=%async_computation.2 | async-start | bytes 5505024 | tf_op jit(solution)/shard_map/all_to_all | solution.py:401
  110.2 1.3 copy-done.12
  111.5 1.6 assemble.5
  113.1 0.9 copy-done.27
  114.0 3.4 %fusion.10 = f32[512,768]{1,0:T(8,128)} fusion(bf16[512,2560]{1,0:T(8,128)(2,1)S(1)} %assemble.5, bf16[1,1,2560,768]{3,2,1,0:T(8,128)(2,1)S(1)} %copy-done.27), kind=kOutput, calls=%fused_computation.16 | convolution fusion | flops 2013265920 | bytes 8126464 | tf_op jit(solution)/shard_map/dot_general | solution.py:526
  117.4 3.3 %fusion.4 = f32[512,768]{1,0:T(8,128)} fusion(bf16[512,2560]{1,0:T(8,128)(2,1)S(1)} %assemble.5, bf16[1,1,2560,768]{3,2,1,0:T(8,128)(2,1)S(1)} %copy-done.29), kind=kOutput, calls=%fused_computation.10 | convolution fusion | flops 2013265920 | bytes 8126464 | tf_op jit(solution)/shard_map/dot_general | solution.py:527
  120.7 1.8 assemble.4
  122.5 0.9 copy-done.25
  123.5 5.3 %multiply_convert_fusion.4 = (bf16[512,768]{1,0:T(8,128)(2,1)S(1)}, bf16[512,768]{1,0:T(8,128)(2,1)S(1)}) fusion(f32[512,768]{1,0:T(8,128)} %fusion.10, f32[512,768]{1,0:T(8,128)} %fusion.4, bf16[512,2560]{1,0:T(8,128)(2,1)S(1)} %assemble.4, bf16[1,1,768,2560]{3,2,1,0:T(8,128)(2,1)S(1)} %copy-done.25), kind=kOutput, calls=%fused_computation.24 | convolution fusion | flops 2018377728 | bytes 11272192 | tf_op jit(solution)/shard_map/dot_general | solution.py:364
  128.8 2.2 %fusion.8 = f32[512,2560]{1,0:T(8,128)S(1)} fusion(bf16[512,768]{1,0:T(8,128)(2,1)S(1)} %get-tuple-element.99, bf16[1,1,2560,768]{3,2,1,0:T(8,128)(2,1)S(1)} %copy-done.27), kind=kOutput, calls=%fused_computation.14 | convolution fusion | flops 2013265920 | bytes 9961472 | tf_op jit(solution)/shard_map/dot_general | solution.py:364
  131.5 2.3 %add_convert_fusion.refs_1_ = bf16[512,2560]{1,0:T(8,128)(2,1)S(1)} fusion(f32[512,2560]{1,0:T(8,128)S(1)} %fusion.8, bf16[512,768]{1,0:T(8,128)(2,1)S(1)} %get-tuple-element.98, bf16[1,1,2560,768]{3,2,1,0:T(8,128)(2,1)S(1)} %copy-done.30), kind=kOutput, calls=%fused_computation.1 | convolution fusion | flops 2015887360 | bytes 12582912 | tf_op jit(solution)/shard_map/dot_general | solution.py:364
  134.5 1.5 copy-done.2
  136.0 1.6 all-to-all-done.2
  137.6 4.4 %all-to-all-start.3 = ((bf16[8,64,2560]{2,1,0:T(8,128)(2,1)}), bf16[8,64,2560]{2,1,0:T(8,128)(2,1)}, u32[]{:S(2)}, u32[]{:S(2)}) async-start(bf16[8,64,2560]{2,1,0:T(8,128)(2,1)} %copy-done.2), calls=%async_computation.3 | async-start | bytes 5242880 | tf_op jit(solution)/shard_map/all_to_all | solution.py:401
  142.0 3.0 %join_forward.1 = bf16[128,2560]{1,0:T(8,128)(2,1)} custom-call(f32[8,128]{1,0:T(8,128)S(1)} %pad_maximum_fusion.refs_1_.refs_0_, bf16[512,2688]{1,0:T(8,128)(2,1)S(1)} %bitcast.87, bf16[128,2560]{1,0:T(8,128)(2,1)S(1)} %bitcast.95), custom_call_target="tpu_custom_call" | custom-call | bytes 4067328 | tf_op jit(solution)/shard_map/join_forward/pallas_call | solution.py:343
  145.0 2.2 %collective-permute-start.14 = (bf16[128,2560]{1,0:T(8,128)(2,1)}, bf16[128,2560]{1,0:T(8,128)(2,1)}, u32[]{:S(2)}, u32[]{:S(2)}) collective-permute-start(bf16[128,2560]{1,0:T(8,128)(2,1)} %join_forward.1), channel_id=1, source_target_pairs={{0,8},{8,16},{16,24},{24,32},{32,40},{40,48},{48,56},{56,64},{64,7... | collective-permute-start | bytes 1966088 | tf_op jit(solution)/shard_map/ppermute | solution.py:26
  148.0 6.3 %convolution_convert_fusion.1 = bf16[2560,768]{1,0:T(8,128)(2,1)} fusion(bf16[512,2560]{1,0:T(8,128)(2,1)} %copy-done.5, bf16[512,768]{1,0:T(8,128)(2,1)} %copy-done.31, f32[512]{0:T(512)S(1)} %select_n.61), kind=kOutput, calls=%fused_computation.3 | convolution fusion | flops 2016411648 | bytes 7342080 | tf_op jit(solution)/shard_map/dot_general | solution.py:358
  154.4 4.2 %convolution_convert_fusion = bf16[2560,768]{1,0:T(8,128)(2,1)} fusion(bf16[512,2560]{1,0:T(8,128)(2,1)S(1)} %copy-done.6, bf16[512,768]{1,0:T(8,128)(2,1)S(1)} %copy-done.35, f32[512]{0:T(512)S(1)} %select_n.61), kind=kOutput, calls=%fused_computation.2 | convolution fusion | flops 2016411648 | bytes 7342080 | tf_op jit(solution)/shard_map/dot_general | solution.py:358
  158.7 4.4 %convolution_convert_fusion.2 = bf16[768,2560]{1,0:T(8,128)(2,1)} fusion(bf16[512,2560]{1,0:T(8,128)(2,1)S(1)} %copy-done.8, f32[512,768]{1,0:T(8,128)S(1)} %copy-done.33, f32[512]{0:T(512)S(1)} %select_n.61, f32[512,768]{1,0:T(8,128)S(1)} %copy-done.32), kind=kOutput, calls=%fused_computation.4 | convolution fusion | flops 2018770944 | bytes 9701376 | tf_op jit(solution)/shard_map/dot_general | solution.py:358
  163.0 4.3 %all-to-all-done.3 = bf16[8,64,2560]{2,1,0:T(8,128)(2,1)} async-done(((bf16[8,64,2560]{2,1,0:T(8,128)(2,1)}), bf16[8,64,2560]{2,1,0:T(8,128)(2,1)}, u32[]{:S(2)}, u32[]{:S(2)}) %all-to-all-start.3) | async-done | bytes 2621472 | tf_op jit(solution)/shard_map/all_to_all | solution.py:401
  167.3 3.3 %join_backward.1 = (bf16[128,2560]{1,0:T(8,128)(2,1)S(1)}, f32[1,2560]{1,0:T(1,128)S(1)}) custom-call(s32[2]{0:T(128)S(1)} %pad_add_fusion.refs_0_.place_ref, f32[8,128]{1,0:T(8,128)S(1)} %pad_maximum_fusion.refs_1_.refs_0_, bf16[512,2560]{1,0:T(8,128)(2,1)} %bitcast.20.refs_2_, bf16[128,2560]{1,0:T(8,128)(2,1)S(1)} %copy-done.4, ...), custom_call_target="tpu_custom_call" | custom-call | bytes 4622856 | tf_op jit(solution)/shard_map/join_backward/pallas_call | solution.py:343
  170.6 3.0 %collective-permute-start.15 = (bf16[128,2560]{1,0:T(8,128)(2,1)S(1)}, bf16[128,2560]{1,0:T(8,128)(2,1)S(1)}, u32[]{:S(2)}, u32[]{:S(2)}) collective-permute-start(bf16[128,2560]{1,0:T(8,128)(2,1)S(1)} %get-tuple-element.94), channel_id=1, source_target_pairs={{8,0},{16,8},{24,16},{32,24},{40,32},{48,40},{56,48},{64,56},{72,6... | collective-permute-start | bytes 1966088 | tf_op jit(solution)/shard_map/ppermute | solution.py:26
  173.6 2.0 %collective-permute-start.16 = (f32[1,2560]{1,0:T(1,128)S(1)}, f32[1,2560]{1,0:T(1,128)S(1)}, u32[]{:S(2)}, u32[]{:S(2)}) collective-permute-start(f32[1,2560]{1,0:T(1,128)S(1)} %get-tuple-element.93.unused_ref), channel_id=1, source_target_pairs={{0,1},{1,0},{2,3},{3,2},{4,5},{5,4},{6,7},{7,6},{8,9},{9,8},{10,11... | collective-permute-start | bytes 30728 | tf_op jit(solution)/shard_map/ppermute | solution.py:579
  175.6 8.6 %collective-permute-done.16 = f32[1,2560]{1,0:T(1,128)S(1)} collective-permute-done((f32[1,2560]{1,0:T(1,128)S(1)}, f32[1,2560]{1,0:T(1,128)S(1)}, u32[]{:S(2)}, u32[]{:S(2)}) %collective-permute-start.16) | collective-permute-done | bytes 10272 | tf_op jit(solution)/shard_map/ppermute | solution.py:579
  184.2 1.6 collective-permute-start.17
  185.7 2.2 %collective-permute-done.17 = f32[1,2560]{1,0:T(1,128)S(1)} collective-permute-done((f32[1,2560]{1,0:T(1,128)S(1)}, f32[1,2560]{1,0:T(1,128)S(1)}, u32[]{:S(2)}, u32[]{:S(2)}) %collective-permute-start.17) | collective-permute-done | bytes 10272 | tf_op jit(solution)/shard_map/ppermute | solution.py:579
  187.9 3.1 %collective-permute-start.18 = (f32[1,2560]{1,0:T(1,128)S(1)}, f32[1,2560]{1,0:T(1,128)S(1)}, u32[]{:S(2)}, u32[]{:S(2)}) collective-permute-start(f32[1,2560]{1,0:T(1,128)S(1)} %add.64), channel_id=1, source_target_pairs={{0,4},{1,5},{2,6},{3,7},{4,0},{5,1},{6,2},{7,3},{8,12},{9,13},{10,... | collective-permute-start | bytes 30728 | tf_op jit(solution)/shard_map/ppermute | solution.py:579
  191.0 2.0 %copy_rows.1 = bf16[128,2560]{1,0:T(8,128)(2,1)} custom-call(bf16[128,2560]{1,0:T(8,128)(2,1)} %collective-permute-done.14.in_ref, f32[1,2560]{1,0:T(1,128)S(1)} %get-tuple-element.93.unused_ref), custom_call_target="tpu_custom_call" | custom-call | bytes 1320960 | tf_op jit(solution)/shard_map/copy_rows/pallas_call | solution.py:343
  193.8 0.8 copy.23
  (103 shorter events, 11.3 us)
Async XLA Ops:
  0.6 31.2 %copy-start.1 = (bf16[1,128,2560]{2,1,0:T(8,128)(2,1)S(1)}, bf16[1,128,2560]{2,1,0:T(8,128)(2,1)}, u32[]{:S(2)}) copy-start(bf16[1,128,2560]{2,1,0:T(8,128)(2,1)} %param.13) | copy-start | bytes 1966084
  0.6 31.2 %copy-start.17 = (f32[1,2560]{1,0:T(1,128)S(1)}, f32[1,2560]{1,0:T(1,128)}, u32[]{:S(2)}) copy-start(f32[1,2560]{1,0:T(1,128)} %refs_6_.1) | copy-start | bytes 30724
  0.7 19.1 %collective-permute-start = (bf16[128,2560]{1,0:T(8,128)(2,1)}, bf16[128,2560]{1,0:T(8,128)(2,1)S(1)}, u32[]{:S(2)}, u32[]{:S(2)}) collective-permute-start(bf16[128,2560]{1,0:T(8,128)(2,1)} %bitcast.91), channel_id=1, source_target_pairs={{0,2},{1,3},{2,4},{3,5},{4,6},{5,7},{6,0},{7,1},{8,10},{9,11},{10,... | collective-permute-start | bytes 1966088 | tf_op jit(solution)/shard_map/ppermute | solution.py:404
  2.6 17.1 %collective-permute-start.1 = (bf16[128,2560]{1,0:T(8,128)(2,1)}, bf16[128,2560]{1,0:T(8,128)(2,1)S(1)}, u32[]{:S(2)}, u32[]{:S(2)}) collective-permute-start(bf16[128,2560]{1,0:T(8,128)(2,1)} %bitcast.92), channel_id=1, source_target_pairs={{0,6},{1,7},{2,0},{3,1},{4,2},{5,3},{6,4},{7,5},{8,14},{9,15},{10,... | collective-permute-start | bytes 1966088 | tf_op jit(solution)/shard_map/ppermute | solution.py:404
  4.8 16.6 %collective-permute-start.2 = (bf16[128,2560]{1,0:T(8,128)(2,1)}, bf16[128,2560]{1,0:T(8,128)(2,1)S(1)}, u32[]{:S(2)}, u32[]{:S(2)}) collective-permute-start(bf16[128,2560]{1,0:T(8,128)(2,1)} %bitcast.96), channel_id=1, source_target_pairs={{0,1},{1,0},{2,3},{3,2},{4,5},{5,4},{6,7},{7,6},{8,9},{9,8},{10,11... | collective-permute-start | bytes 1966088 | tf_op jit(solution)/shard_map/ppermute | solution.py:404
  8.8 18.8 %all-to-all-start = ((f32[8,8,128]{2,1,0:T(8,128)}), f32[8,8,128]{2,1,0:T(8,128)S(1)}, u32[]{:S(2)}, u32[]{:S(2)}) async-start(f32[8,8,128]{2,1,0:T(8,128)} %broadcast_in_dim.37), calls=%async_computation | async-start | bytes 65536 | tf_op jit(solution)/shard_map/all_to_all | solution.py:401
  21.4 1.5 copy-start.20
  22.2 20.8 %copy-start.22 = (f32[2560]{0:T(1024)S(1)}, f32[2560]{0:T(1024)}, u32[]{:S(2)}) copy-start(f32[2560]{0:T(1024)} %param.24) | copy-start | bytes 30724
  22.2 20.9 %copy-start.13 = (bf16[1,128,2560]{2,1,0:T(8,128)(2,1)S(1)}, bf16[1,128,2560]{2,1,0:T(8,128)(2,1)}, u32[]{:S(2)}) copy-start(bf16[1,128,2560]{2,1,0:T(8,128)(2,1)} %param.15) | copy-start | bytes 1966084
  22.2 9.6 %collective-permute-start.3 = (bf16[64,2560]{1,0:T(8,128)(2,1)}, bf16[64,2560]{1,0:T(8,128)(2,1)}, u32[]{:S(2)}, u32[]{:S(2)}) collective-permute-start(bf16[64,2560]{1,0:T(8,128)(2,1)} %slice.15), channel_id=1, source_target_pairs={{0,2},{1,3},{2,4},{3,5},{4,6},{5,7},{6,0},{7,1},{8,10},{9,11},{10,... | collective-permute-start | bytes 983048 | tf_op jit(solution)/shard_map/ppermute | solution.py:404
  23.0 8.9 %collective-permute-start.4 = (bf16[64,2560]{1,0:T(8,128)(2,1)}, bf16[64,2560]{1,0:T(8,128)(2,1)}, u32[]{:S(2)}, u32[]{:S(2)}) collective-permute-start(bf16[64,2560]{1,0:T(8,128)(2,1)} %slice.16), channel_id=1, source_target_pairs={{0,6},{1,7},{2,0},{3,1},{4,2},{5,3},{6,4},{7,5},{8,14},{9,15},{10,... | collective-permute-start | bytes 983048 | tf_op jit(solution)/shard_map/ppermute | solution.py:404
  27.6 37.3 %copy-start.3 = (bf16[128,2560]{1,0:T(8,128)(2,1)}, bf16[128,2560]{1,0:T(8,128)(2,1)S(1)}, u32[]{:S(2)}) copy-start(bf16[128,2560]{1,0:T(8,128)(2,1)S(1)} %bitcast_select_fusion.own_ref.refs_3_) | copy-start | bytes 1966084
  27.7 15.4 %copy-start.21 = (bf16[128,2560]{1,0:T(8,128)(2,1)S(1)}, bf16[128,2560]{1,0:T(8,128)(2,1)}, u32[]{:S(2)}) copy-start(bf16[128,2560]{1,0:T(8,128)(2,1)} %copy-done.20) | copy-start | bytes 1966084
  37.1 1.1 copy-start.9
  38.2 38.6 %collective-permute-start.13 = (bf16[256,2560]{1,0:T(8,128)(2,1)}, bf16[256,2560]{1,0:T(8,128)(2,1)}, u32[]{:S(2)}, u32[]{:S(2)}) collective-permute-start(bf16[256,2560]{1,0:T(8,128)(2,1)} %get-tuple-element.78), channel_id=1, source_target_pairs={{0,1},{1,0},{2,3},{3,2},{4,5},{5,4},{6,7},{7,6},{8,9},{9,8},{10,11... | collective-permute-start | bytes 3932168 | tf_op jit(solution)/shard_map/ppermute | solution.py:404
  39.4 15.6 %collective-permute-start.5 = (bf16[128,2560]{1,0:T(8,128)(2,1)S(1)}, bf16[128,2560]{1,0:T(8,128)(2,1)S(1)}, u32[]{:S(2)}, u32[]{:S(2)}) collective-permute-start(bf16[128,2560]{1,0:T(8,128)(2,1)S(1)} %bitcast_select_fusion.own_ref.refs_3_), channel_id=1, source_target_pairs={{0,2},{1,3},{2,4},{3,5},{4,6},{5,7},{6,0},{7,1},{8,10},{9,11},{10,... | collective-permute-start | bytes 1966088 | tf_op jit(solution)/shard_map/ppermute | solution.py:404
  40.1 14.8 %collective-permute-start.6 = (bf16[128,2560]{1,0:T(8,128)(2,1)S(1)}, bf16[128,2560]{1,0:T(8,128)(2,1)S(1)}, u32[]{:S(2)}, u32[]{:S(2)}) collective-permute-start(bf16[128,2560]{1,0:T(8,128)(2,1)S(1)} %bitcast_select_fusion.own_ref.refs_3_), channel_id=1, source_target_pairs={{0,6},{1,7},{2,0},{3,1},{4,2},{5,3},{6,4},{7,5},{8,14},{9,15},{10,... | collective-permute-start | bytes 1966088 | tf_op jit(solution)/shard_map/ppermute | solution.py:404
  48.3 0.8 copy-start.15
  55.7 8.5 %collective-permute-start.7 = (bf16[64,2560]{1,0:T(8,128)(2,1)}, bf16[64,2560]{1,0:T(8,128)(2,1)S(1)}, u32[]{:S(2)}, u32[]{:S(2)}) collective-permute-start(bf16[64,2560]{1,0:T(8,128)(2,1)} %slice.17), channel_id=1, source_target_pairs={{0,2},{1,3},{2,4},{3,5},{4,6},{5,7},{6,0},{7,1},{8,10},{9,11},{10,... | collective-permute-start | bytes 983048 | tf_op jit(solution)/shard_map/ppermute | solution.py:404
  57.6 7.3 %collective-permute-start.8 = (bf16[64,2560]{1,0:T(8,128)(2,1)}, bf16[64,2560]{1,0:T(8,128)(2,1)S(1)}, u32[]{:S(2)}, u32[]{:S(2)}) collective-permute-start(bf16[64,2560]{1,0:T(8,128)(2,1)} %slice.18), channel_id=1, source_target_pairs={{0,6},{1,7},{2,0},{3,1},{4,2},{5,3},{6,4},{7,5},{8,14},{9,15},{10,... | collective-permute-start | bytes 983048 | tf_op jit(solution)/shard_map/ppermute | solution.py:404
  59.8 17.0 %copy-start.10 = (bf16[256,2560]{1,0:T(8,128)(2,1)S(1)}, bf16[256,2560]{1,0:T(8,128)(2,1)}, u32[]{:S(2)}) copy-start(bf16[256,2560]{1,0:T(8,128)(2,1)} %copy-done.9) | copy-start | bytes 3932164
  69.6 1.1 copy-start.11
  70.6 35.7 %collective-permute-start.9 = (bf16[128,2560]{1,0:T(8,128)(2,1)}, bf16[128,2560]{1,0:T(8,128)(2,1)}, u32[]{:S(2)}, u32[]{:S(2)}) collective-permute-start(bf16[128,2560]{1,0:T(8,128)(2,1)} %get-tuple-element.69), channel_id=1, source_target_pairs={{0,2},{1,3},{2,4},{3,5},{4,6},{5,7},{6,0},{7,1},{8,10},{9,11},{10,... | collective-permute-start | bytes 1966088 | tf_op jit(solution)/shard_map/ppermute | solution.py:404
  72.4 33.9 %collective-permute-start.10 = (bf16[128,2560]{1,0:T(8,128)(2,1)}, bf16[128,2560]{1,0:T(8,128)(2,1)}, u32[]{:S(2)}, u32[]{:S(2)}) collective-permute-start(bf16[128,2560]{1,0:T(8,128)(2,1)} %get-tuple-element.70), channel_id=1, source_target_pairs={{0,6},{1,7},{2,0},{3,1},{4,2},{5,3},{6,4},{7,5},{8,14},{9,15},{10,... | collective-permute-start | bytes 1966088 | tf_op jit(solution)/shard_map/ppermute | solution.py:404
  73.9 32.4 %collective-permute-start.11 = (bf16[128,2560]{1,0:T(8,128)(2,1)}, bf16[128,2560]{1,0:T(8,128)(2,1)}, u32[]{:S(2)}, u32[]{:S(2)}) collective-permute-start(bf16[128,2560]{1,0:T(8,128)(2,1)} %get-tuple-element.71), channel_id=1, source_target_pairs={{0,4},{1,5},{2,6},{3,7},{4,0},{5,1},{6,2},{7,3},{8,12},{9,13},{10,... | collective-permute-start | bytes 1966088 | tf_op jit(solution)/shard_map/ppermute | solution.py:404
  75.9 30.4 %collective-permute-start.12 = (bf16[256,2560]{1,0:T(8,128)(2,1)}, bf16[256,2560]{1,0:T(8,128)(2,1)}, u32[]{:S(2)}, u32[]{:S(2)}) collective-permute-start(bf16[256,2560]{1,0:T(8,128)(2,1)} %get-tuple-element.72), channel_id=1, source_target_pairs={{0,1},{1,0},{2,3},{3,2},{4,5},{5,4},{6,7},{7,6},{8,9},{9,8},{10,11... | collective-permute-start | bytes 3932168 | tf_op jit(solution)/shard_map/ppermute | solution.py:404
  76.8 2.5 %copy-start.26 = (bf16[1,1,2560,768]{3,2,1,0:T(8,128)(2,1)S(1)}, bf16[1,1,2560,768]{3,2,1,0:T(8,128)(2,1)}, u32[]{:S(2)}) copy-start(bf16[1,1,2560,768]{3,2,1,0:T(8,128)(2,1)} %param.20) | copy-start | bytes 11796484
  79.3 2.2 %copy-start.28 = (bf16[1,1,2560,768]{3,2,1,0:T(8,128)(2,1)S(1)}, bf16[1,1,2560,768]{3,2,1,0:T(8,128)(2,1)}, u32[]{:S(2)}) copy-start(bf16[1,1,2560,768]{3,2,1,0:T(8,128)(2,1)} %param.21) | copy-start | bytes 11796484
  81.5 2.3 %copy-start.24 = (bf16[1,1,768,2560]{3,2,1,0:T(8,128)(2,1)S(1)}, bf16[1,1,768,2560]{3,2,1,0:T(8,128)(2,1)}, u32[]{:S(2)}) copy-start(bf16[1,1,768,2560]{3,2,1,0:T(8,128)(2,1)} %param.22) | copy-start | bytes 11796484
  86.0 5.4 %copy-start.23 = (s32[128]{0:T(128)S(1)}, s32[128]{0:T(128)}, u32[]{:S(2)}) copy-start(s32[128]{0:T(128)} %param.25) | copy-start | bytes 1540
  88.0 14.2 %all-to-all-start.1 = ((f32[8,1,64]{2,1,0:T(1,128)}), f32[8,1,64]{2,1,0:T(1,128)S(1)}, u32[]{:S(2)}, u32[]{:S(2)}) async-start(f32[8,1,64]{2,1,0:T(1,128)} %get-tuple-element.79), calls=%async_computation.1 | async-start | bytes 8192 | tf_op jit(solution)/shard_map/all_to_all | solution.py:401
  104.1 1.5 copy-start
  105.7 0.6 copy-start.18
  106.3 31.2 %all-to-all-start.2 = ((bf16[8,64,2688]{2,1,0:T(8,128)(2,1)}), bf16[8,64,2688]{2,1,0:T(8,128)(2,1)S(1)}, u32[]{:S(2)}, u32[]{:S(2)}) async-start(bf16[8,64,2688]{2,1,0:T(8,128)(2,1)} %bitcast.90), calls=%async_computation.2 | async-start | bytes 5505024 | tf_op jit(solution)/shard_map/all_to_all | solution.py:401
  110.2 1.3 copy-start.12
  111.5 2.5 %copy-start.27 = (bf16[1,1,2560,768]{3,2,1,0:T(8,128)(2,1)S(1)}, bf16[1,1,2560,768]{3,2,1,0:T(8,128)(2,1)}, u32[]{:S(2)}) copy-start(bf16[1,1,2560,768]{3,2,1,0:T(8,128)(2,1)} %param.20) | copy-start | bytes 11796484
  114.0 3.4 %copy-start.5 = (bf16[512,2560]{1,0:T(8,128)(2,1)}, bf16[512,2560]{1,0:T(8,128)(2,1)S(1)}, u32[]{:S(2)}) copy-start(bf16[512,2560]{1,0:T(8,128)(2,1)S(1)} %assemble.5) | copy-start | bytes 7864324
  114.0 3.4 %copy-start.29 = (bf16[1,1,2560,768]{3,2,1,0:T(8,128)(2,1)S(1)}, bf16[1,1,2560,768]{3,2,1,0:T(8,128)(2,1)}, u32[]{:S(2)}) copy-start(bf16[1,1,2560,768]{3,2,1,0:T(8,128)(2,1)} %param.21) | copy-start | bytes 11796484
  117.4 3.3 %copy-start.16 = (bf16[128,2560]{1,0:T(8,128)(2,1)S(1)}, bf16[128,2560]{1,0:T(8,128)(2,1)}, u32[]{:S(2)}) copy-start(bf16[128,2560]{1,0:T(8,128)(2,1)} %copy-done.15) | copy-start | bytes 1966084
  120.7 2.7 %copy-start.25 = (bf16[1,1,768,2560]{3,2,1,0:T(8,128)(2,1)S(1)}, bf16[1,1,768,2560]{3,2,1,0:T(8,128)(2,1)}, u32[]{:S(2)}) copy-start(bf16[1,1,768,2560]{3,2,1,0:T(8,128)(2,1)} %param.22) | copy-start | bytes 11796484
  123.5 5.4 %copy-start.7 = (bf16[512,2560]{1,0:T(8,128)(2,1)}, bf16[512,2560]{1,0:T(8,128)(2,1)S(1)}, u32[]{:S(2)}) copy-start(bf16[512,2560]{1,0:T(8,128)(2,1)S(1)} %assemble.4) | copy-start | bytes 7864324
  128.8 2.3 %copy-start.31 = (bf16[512,768]{1,0:T(8,128)(2,1)}, bf16[512,768]{1,0:T(8,128)(2,1)S(1)}, u32[]{:S(2)}) copy-start(bf16[512,768]{1,0:T(8,128)(2,1)S(1)} %get-tuple-element.99) | copy-start | bytes 2359300
  128.8 2.3 %copy-start.34 = (bf16[512,768]{1,0:T(8,128)(2,1)}, bf16[512,768]{1,0:T(8,128)(2,1)S(1)}, u32[]{:S(2)}) copy-start(bf16[512,768]{1,0:T(8,128)(2,1)S(1)} %get-tuple-element.98) | copy-start | bytes 2359300
  128.8 2.7 %copy-start.30 = (bf16[1,1,2560,768]{3,2,1,0:T(8,128)(2,1)S(1)}, bf16[1,1,2560,768]{3,2,1,0:T(8,128)(2,1)}, u32[]{:S(2)}) copy-start(bf16[1,1,2560,768]{3,2,1,0:T(8,128)(2,1)} %param.21) | copy-start | bytes 11796484
  134.5 1.5 copy-start.2
  137.6 29.7 %all-to-all-start.3 = ((bf16[8,64,2560]{2,1,0:T(8,128)(2,1)}), bf16[8,64,2560]{2,1,0:T(8,128)(2,1)}, u32[]{:S(2)}, u32[]{:S(2)}) async-start(bf16[8,64,2560]{2,1,0:T(8,128)(2,1)} %copy-done.2), calls=%async_computation.3 | async-start | bytes 5242880 | tf_op jit(solution)/shard_map/all_to_all | solution.py:401
  145.0 46.1 %collective-permute-start.14 = (bf16[128,2560]{1,0:T(8,128)(2,1)}, bf16[128,2560]{1,0:T(8,128)(2,1)}, u32[]{:S(2)}, u32[]{:S(2)}) collective-permute-start(bf16[128,2560]{1,0:T(8,128)(2,1)} %join_forward.1), channel_id=1, source_target_pairs={{0,8},{8,16},{16,24},{24,32},{32,40},{40,48},{48,56},{56,64},{64,7... | collective-permute-start | bytes 1966088 | tf_op jit(solution)/shard_map/ppermute | solution.py:26
  148.0 6.3 %copy-start.6 = (bf16[512,2560]{1,0:T(8,128)(2,1)S(1)}, bf16[512,2560]{1,0:T(8,128)(2,1)}, u32[]{:S(2)}) copy-start(bf16[512,2560]{1,0:T(8,128)(2,1)} %copy-done.5) | copy-start | bytes 7864324
  148.0 6.3 %copy-start.35 = (bf16[512,768]{1,0:T(8,128)(2,1)S(1)}, bf16[512,768]{1,0:T(8,128)(2,1)}, u32[]{:S(2)}) copy-start(bf16[512,768]{1,0:T(8,128)(2,1)} %copy-done.34) | copy-start | bytes 2359300
  154.4 4.3 %copy-start.8 = (bf16[512,2560]{1,0:T(8,128)(2,1)S(1)}, bf16[512,2560]{1,0:T(8,128)(2,1)}, u32[]{:S(2)}) copy-start(bf16[512,2560]{1,0:T(8,128)(2,1)} %copy-done.7) | copy-start | bytes 7864324
  154.4 4.3 %copy-start.32 = (f32[512,768]{1,0:T(8,128)S(1)}, f32[512,768]{1,0:T(8,128)}, u32[]{:S(2)}) copy-start(f32[512,768]{1,0:T(8,128)} %fusion.10) | copy-start | bytes 4718596
  154.4 4.3 %copy-start.33 = (f32[512,768]{1,0:T(8,128)S(1)}, f32[512,768]{1,0:T(8,128)}, u32[]{:S(2)}) copy-start(f32[512,768]{1,0:T(8,128)} %fusion.4) | copy-start | bytes 4718596
  158.6 8.7 %copy-start.4 = (bf16[128,2560]{1,0:T(8,128)(2,1)S(1)}, bf16[128,2560]{1,0:T(8,128)(2,1)}, u32[]{:S(2)}) copy-start(bf16[128,2560]{1,0:T(8,128)(2,1)} %copy-done.3) | copy-start | bytes 1966084
  158.6 8.6 %copy-start.14 = (bf16[1,128,2560]{2,1,0:T(8,128)(2,1)S(1)}, bf16[1,128,2560]{2,1,0:T(8,128)(2,1)}, u32[]{:S(2)}) copy-start(bf16[1,128,2560]{2,1,0:T(8,128)(2,1)} %param.15) | copy-start | bytes 1966084
  158.7 8.6 %copy-start.19 = (f32[128,1]{1,0:T(8,128)S(1)}, f32[128,1]{1,0:T(8,128)}, u32[]{:S(2)}) copy-start(f32[128,1]{1,0:T(8,128)} %copy-done.18) | copy-start | bytes 1540
  170.6 23.2 %collective-permute-start.15 = (bf16[128,2560]{1,0:T(8,128)(2,1)S(1)}, bf16[128,2560]{1,0:T(8,128)(2,1)S(1)}, u32[]{:S(2)}, u32[]{:S(2)}) collective-permute-start(bf16[128,2560]{1,0:T(8,128)(2,1)S(1)} %get-tuple-element.94), channel_id=1, source_target_pairs={{8,0},{16,8},{24,16},{32,24},{40,32},{48,40},{56,48},{64,56},{72,6... | collective-permute-start | bytes 1966088 | tf_op jit(solution)/shard_map/ppermute | solution.py:26
  173.6 10.5 %collective-permute-start.16 = (f32[1,2560]{1,0:T(1,128)S(1)}, f32[1,2560]{1,0:T(1,128)S(1)}, u32[]{:S(2)}, u32[]{:S(2)}) collective-permute-start(f32[1,2560]{1,0:T(1,128)S(1)} %get-tuple-element.93.unused_ref), channel_id=1, source_target_pairs={{0,1},{1,0},{2,3},{3,2},{4,5},{5,4},{6,7},{7,6},{8,9},{9,8},{10,11... | collective-permute-start | bytes 30728 | tf_op jit(solution)/shard_map/ppermute | solution.py:579
  184.2 3.8 %collective-permute-start.17 = (f32[1,2560]{1,0:T(1,128)S(1)}, f32[1,2560]{1,0:T(1,128)S(1)}, u32[]{:S(2)}, u32[]{:S(2)}) collective-permute-start(f32[1,2560]{1,0:T(1,128)S(1)} %add.63), channel_id=1, source_target_pairs={{0,2},{1,3},{2,0},{3,1},{4,6},{5,7},{6,4},{7,5},{8,10},{9,11},{10,... | collective-permute-start | bytes 30728 | tf_op jit(solution)/shard_map/ppermute | solution.py:579
  187.9 5.3 %collective-permute-start.18 = (f32[1,2560]{1,0:T(1,128)S(1)}, f32[1,2560]{1,0:T(1,128)S(1)}, u32[]{:S(2)}, u32[]{:S(2)}) collective-permute-start(f32[1,2560]{1,0:T(1,128)S(1)} %add.64), channel_id=1, source_target_pairs={{0,4},{1,5},{2,6},{3,7},{4,0},{5,1},{6,2},{7,3},{8,12},{9,13},{10,... | collective-permute-start | bytes 30728 | tf_op jit(solution)/shard_map/ppermute | solution.py:579
where the time goes:
time: 195 us
  waiting for transfers between devices  51.5 us (26%)
  starting transfers between devices  49.9 us (26%)
  matrix products  38.1 us (20%)
  Pallas kernels  33 us (17%)
  local copies, waits for them, and re-layouts  16.7 us (9%)
  other arithmetic  4.41 us (2%)
    pallas_call x12, Pallas kernels, call(): pl.pallas_call(kernel, cost_estimate=pl.CostEstimate(flops=flops, transce...  33 us
    ppermute x14, waiting for transfers between devices, move(): lax.ppermute(value, 'expert', [(source, (source + 2 * dz) % groups ^ dx)...  24.2 us
    ppermute x14, starting transfers between devices, move(): lax.ppermute(value, 'expert', [(source, (source + 2 * dz) % groups ^ dx)...  22.9 us
    all_to_all x4, waiting for transfers between devices, exchange(): lax.all_to_all(value, 'expert', split_axis=0, concat_axis=0, tiled=True)  16.3 us
    all_to_all x4, starting transfers between devices, exchange(): lax.all_to_all(value, 'expert', split_axis=0, concat_axis=0, tiled=True)  15.2 us
    dot_general x3, matrix products, contract_rows(): lax.dot_general(left_op, right_op, (((0,), (0,)), ((), ())), preferred_el...  14.9 us
    unnamed x73, local copies, waits for them, and re-layouts  12 us
    ppermute x3, waiting for transfers between devices, on_device(): lax.ppermute(gain_grad, 'expert', [(source, source ^ step) for source in...  11 us
  transfers between devices with their start and end apart: 23, of which 12 were waited for; matrix products, arithmetic and copies ran while one was open for 24% of the time, Pallas kernels for 14%

commit v1 on v0

--- a/solution.py
+++ b/solution.py
@@ -574,12 +574,12 @@
         copy_rows, "copy_rows", [((tok_dev, width), bf16)], (next_input, gain_local), [vmem] * 2
     )
     gain_grad = gain_local
-    step = 1
-    while step < groups:
+    step = groups // 2
+    while step:
         gain_grad = gain_grad + lax.ppermute(
             gain_grad, "expert", [(source, source ^ step) for source in range(groups)]
         )
-        step *= 2
+        step //= 2
     return (
         next_input[None],
         prev_grad[None],

time: 195 us -> 195 us (level)
  the two profiles are of different devices: /device:TPU:4 before, /device:TPU:24 now
where the time goes in v1:
time: 195 us; the launch traced here: 194 us
  waiting for transfers between devices  57.1 us (29%)
  starting transfers between devices  43.7 us (22%)
  matrix products  38.1 us (20%)
  Pallas kernels  33 us (17%)
  local copies, waits for them, and re-layouts  16.7 us (9%)
  other arithmetic  4.41 us (2%)
    pallas_call x12, Pallas kernels, call(): pl.pallas_call(kernel, cost_estimate=pl.CostEstimate(flops=flops, transce...  33 us
    ppermute x14, waiting for transfers between devices, move(): lax.ppermute(value, 'expert', [(source, (source + 2 * dz) % groups ^ dx)...  24 us
    all_to_all x4, waiting for transfers between devices, exchange(): lax.all_to_all(value, 'expert', split_axis=0, concat_axis=0, tiled=True)  23.3 us
    ppermute x14, starting transfers between devices, move(): lax.ppermute(value, 'expert', [(source, (source + 2 * dz) % groups ^ dx)...  23.2 us
    all_to_all x4, starting transfers between devices, exchange(): lax.all_to_all(value, 'expert', split_axis=0, concat_axis=0, tiled=True)  15.4 us
    dot_general x3, matrix products, contract_rows(): lax.dot_general(left_op, right_op, (((0,), (0,)), ((), ())), preferred_el...  14.9 us
    unnamed x73, local copies, waits for them, and re-layouts  12 us
    dot_general x3, matrix products, contract_cols(): lax.dot_general(left_op, right_op, (((1,), (1,)), ((), ())), preferred_el...  9.83 us
  transfers between devices with their start and end apart: 23, of which 12 were waited for; matrix products, arithmetic and copies ran while one was open for 24% of the time, Pallas kernels for 14%

profile of v1, /device:TPU:24, one launch (start us, length us, event | category | flops | bytes accessed | tf_op | source)
XLA Modules:
  0.0 194.0 jit_solution(7420468822189219269)
XLA Ops:
  0.7 2.0 %collective-permute-start = (bf16[128,2560]{1,0:T(8,128)(2,1)}, bf16[128,2560]{1,0:T(8,128)(2,1)S(1)}, u32[]{:S(2)}, u32[]{:S(2)}) collective-permute-start(bf16[128,2560]{1,0:T(8,128)(2,1)} %bitcast.91), channel_id=1, source_target_pairs={{0,2},{1,3},{2,4},{3,5},{4,6},{5,7},{6,0},{7,1},{8,10},{9,11},{10,... | collective-permute-start | bytes 1966088 | tf_op jit(solution)/shard_map/ppermute | solution.py:404
  2.6 2.2 %collective-permute-start.1 = (bf16[128,2560]{1,0:T(8,128)(2,1)}, bf16[128,2560]{1,0:T(8,128)(2,1)S(1)}, u32[]{:S(2)}, u32[]{:S(2)}) collective-permute-start(bf16[128,2560]{1,0:T(8,128)(2,1)} %bitcast.92), channel_id=1, source_target_pairs={{0,6},{1,7},{2,0},{3,1},{4,2},{5,3},{6,4},{7,5},{8,14},{9,15},{10,... | collective-permute-start | bytes 1966088 | tf_op jit(solution)/shard_map/ppermute | solution.py:404
  4.8 1.5 collective-permute-start.2
  9.1 3.3 %all-to-all-start = ((f32[8,8,128]{2,1,0:T(8,128)}), f32[8,8,128]{2,1,0:T(8,128)S(1)}, u32[]{:S(2)}, u32[]{:S(2)}) async-start(f32[8,8,128]{2,1,0:T(8,128)} %broadcast_in_dim.37), calls=%async_computation | async-start | bytes 65536 | tf_op jit(solution)/shard_map/all_to_all | solution.py:401
  12.5 7.3 %collective-permute-done.below_ref = bf16[128,2560]{1,0:T(8,128)(2,1)S(1)} collective-permute-done((bf16[128,2560]{1,0:T(8,128)(2,1)}, bf16[128,2560]{1,0:T(8,128)(2,1)S(1)}, u32[]{:S(2)}, u32[]{:S(2)}) %collective-permute-start) | collective-permute-done | bytes 655392 | tf_op jit(solution)/shard_map/ppermute | solution.py:404
  19.8 1.7 collective-permute-done.2.refs_3_
  21.4 0.8 slice.15
  23.0 3.2 %collective-permute-start.4 = (bf16[64,2560]{1,0:T(8,128)(2,1)}, bf16[64,2560]{1,0:T(8,128)(2,1)}, u32[]{:S(2)}, u32[]{:S(2)}) collective-permute-start(bf16[64,2560]{1,0:T(8,128)(2,1)} %slice.16), channel_id=1, source_target_pairs={{0,6},{1,7},{2,0},{3,1},{4,2},{5,3},{6,4},{7,5},{8,14},{9,15},{10,... | collective-permute-start | bytes 983048 | tf_op jit(solution)/shard_map/ppermute | solution.py:404
  26.2 1.4 bitcast_select_fusion.own_ref.refs_3_
  27.7 4.2 %collective-permute-done.3.far_low_ref = bf16[64,2560]{1,0:T(8,128)(2,1)} collective-permute-done((bf16[64,2560]{1,0:T(8,128)(2,1)}, bf16[64,2560]{1,0:T(8,128)(2,1)}, u32[]{:S(2)}, u32[]{:S(2)}) %collective-permute-start.3) | collective-permute-done | bytes 327712 | tf_op jit(solution)/shard_map/ppermute | solution.py:404
  31.8 5.3 %pick_rows.3 = (bf16[256,2560]{1,0:T(8,128)(2,1)S(1)}, bf16[256,2560]{1,0:T(8,128)(2,1)}) custom-call(s32[2]{0:T(128)S(1)} %pad_add_fusion.refs_0_.place_ref, f32[8,8,128]{2,1,0:T(8,128)S(1)} %all-to-all-done.refs_1_.table_ref, bf16[128,2560]{1,0:T(8,128)(2,1)S(1)} %bitcast.93, bf16[128,2560]{1,0:T(8,128)(2,1)S(1)} %collective-permute-done.below_ref, ...), custom_call_target="tpu_custom_call" | custom-call | flops 671088640 | bytes 5285896 | tf_op jit(solution)/shard_map/pick_rows/pallas_call | solution.py:343
  37.1 1.1 copy-done.9
  38.2 1.5 collective-permute-start.13
  39.7 0.8 collective-permute-start.5
  40.4 2.9 %collective-permute-start.6 = (bf16[128,2560]{1,0:T(8,128)(2,1)S(1)}, bf16[128,2560]{1,0:T(8,128)(2,1)S(1)}, u32[]{:S(2)}, u32[]{:S(2)}) collective-permute-start(bf16[128,2560]{1,0:T(8,128)(2,1)S(1)} %bitcast_select_fusion.own_ref.refs_3_), channel_id=1, source_target_pairs={{0,6},{1,7},{2,0},{3,1},{4,2},{5,3},{6,4},{7,5},{8,14},{9,15},{10,... | collective-permute-start | bytes 1966088 | tf_op jit(solution)/shard_map/ppermute | solution.py:404
  43.4 5.2 %weigh_rows.1 = (bf16[128,2560]{1,0:T(8,128)(2,1)S(1)}, bf16[128,2560]{1,0:T(8,128)(2,1)}, bf16[128,2560]{1,0:T(8,128)(2,1)}, bf16[128,2560]{1,0:T(8,128)(2,1)}) custom-call(s32[2]{0:T(128)S(1)} %pad_add_fusion.refs_0_.place_ref, f32[8,8,128]{2,1,0:T(8,128)S(1)} %all-to-all-done.refs_1_.table_ref, bf16[128,2560]{1,0:T(8,128)(2,1)S(1)} %bitcast.97, ...), custom_call_target="tpu_custom_call" | custom-call | flops 1342177280 | bytes 3975176 | tf_op jit(solution)/shard_map/weigh_rows/pallas_call | solution.py:343
  48.6 0.8 copy-done.15
  49.4 5.8 %collective-permute-done.5.below_ref = bf16[128,2560]{1,0:T(8,128)(2,1)S(1)} collective-permute-done((bf16[128,2560]{1,0:T(8,128)(2,1)S(1)}, bf16[128,2560]{1,0:T(8,128)(2,1)S(1)}, u32[]{:S(2)}, u32[]{:S(2)}) %collective-permute-start.5) | collective-permute-done | bytes 655392 | tf_op jit(solution)/shard_map/ppermute | solution.py:404
  56.0 1.1 collective-permute-start.7
  57.9 2.1 %collective-permute-start.8 = (bf16[64,2560]{1,0:T(8,128)(2,1)}, bf16[64,2560]{1,0:T(8,128)(2,1)S(1)}, u32[]{:S(2)}, u32[]{:S(2)}) collective-permute-start(bf16[64,2560]{1,0:T(8,128)(2,1)} %slice.18), channel_id=1, source_target_pairs={{0,6},{1,7},{2,0},{3,1},{4,2},{5,3},{6,4},{7,5},{8,14},{9,15},{10,... | collective-permute-start | bytes 983048 | tf_op jit(solution)/shard_map/ppermute | solution.py:404
  60.1 4.4 %collective-permute-done.7.far_low_ref = bf16[64,2560]{1,0:T(8,128)(2,1)S(1)} collective-permute-done((bf16[64,2560]{1,0:T(8,128)(2,1)}, bf16[64,2560]{1,0:T(8,128)(2,1)S(1)}, u32[]{:S(2)}, u32[]{:S(2)}) %collective-permute-start.7) | collective-permute-done | bytes 327712 | tf_op jit(solution)/shard_map/ppermute | solution.py:404
  65.1 4.7 %pick_rows.2 = (bf16[256,2560]{1,0:T(8,128)(2,1)S(1)}, bf16[256,2560]{1,0:T(8,128)(2,1)}) custom-call(s32[2]{0:T(128)S(1)} %pad_add_fusion.refs_0_.place_ref, f32[8,8,128]{2,1,0:T(8,128)S(1)} %all-to-all-done.refs_1_.table_ref, bf16[128,2560]{1,0:T(8,128)(2,1)S(1)} %bitcast_select_fusion.own_ref.refs_3_, ...), custom_call_target="tpu_custom_call" | custom-call | flops 671088640 | bytes 5285896 | tf_op jit(solution)/shard_map/pick_rows/pallas_call | solution.py:343
  69.9 1.1 copy-done.11
  70.9 1.7 collective-permute-start.9
  72.7 1.6 collective-permute-start.10
  74.2 2.0 %collective-permute-start.11 = (bf16[128,2560]{1,0:T(8,128)(2,1)}, bf16[128,2560]{1,0:T(8,128)(2,1)}, u32[]{:S(2)}, u32[]{:S(2)}) collective-permute-start(bf16[128,2560]{1,0:T(8,128)(2,1)} %get-tuple-element.71), channel_id=1, source_target_pairs={{0,4},{1,5},{2,6},{3,7},{4,0},{5,1},{6,2},{7,3},{8,12},{9,13},{10,... | collective-permute-start | bytes 1966088 | tf_op jit(solution)/shard_map/ppermute | solution.py:404
  76.8 1.6 assemble.3
  78.4 0.9 copy-done.26
  79.3 2.2 %fusion.12 = f32[512,768]{1,0:T(8,128)S(1)} fusion(bf16[512,2560]{1,0:T(8,128)(2,1)S(1)} %assemble.3, bf16[1,1,2560,768]{3,2,1,0:T(8,128)(2,1)S(1)} %copy-done.26), kind=kOutput, calls=%fused_computation.18 | convolution fusion | flops 2013265920 | bytes 8126464 | tf_op jit(solution)/shard_map/dot_general | solution.py:490
  81.5 2.3 %multiply_convert_fusion.6 = bf16[512,768]{1,0:T(8,128)(2,1)S(1)} fusion(f32[512,768]{1,0:T(8,128)S(1)} %fusion.12, bf16[512,2560]{1,0:T(8,128)(2,1)S(1)} %assemble.3, bf16[1,1,2560,768]{3,2,1,0:T(8,128)(2,1)S(1)} %copy-done.28), kind=kOutput, calls=%fused_computation.28 | convolution fusion | flops 2015625216 | bytes 8912896 | tf_op jit(solution)/shard_map/dot_general | solution.py:491
  83.8 2.2 %convolution_convert_fusion.3.refs_1_ = bf16[512,2560]{1,0:T(8,128)(2,1)S(1)} fusion(bf16[512,768]{1,0:T(8,128)(2,1)S(1)} %multiply_convert_fusion.6, bf16[1,1,768,2560]{3,2,1,0:T(8,128)(2,1)S(1)} %copy-done.24), kind=kOutput, calls=%fused_computation.5 | convolution fusion | flops 2014576640 | bytes 7340032 | tf_op jit(solution)/shard_map/dot_general | solution.py:493
  86.0 2.0 %attach_dots.1 = (bf16[8,64,2688]{2,1,0:T(8,128)(2,1)S(1)}, f32[8,1,64]{2,1,0:T(1,128)}) custom-call(s32[2]{0:T(128)S(1)} %pad_add_fusion.refs_0_.place_ref, bf16[512,2560]{1,0:T(8,128)(2,1)S(1)} %convolution_convert_fusion.3.refs_1_, f32[1,2560]{1,0:T(1,128)S(1)} %broadcast_in_dim.38.refs_4_.refs_2_.refs_3_.refs_7_), custom_call_target="tpu_custom_call" | custom-call | bytes 5386248 | tf_op jit(solution)/shard_map/attach_dots/pallas_call | solution.py:343
  88.0 3.7 %all-to-all-start.1 = ((f32[8,1,64]{2,1,0:T(1,128)}), f32[8,1,64]{2,1,0:T(1,128)S(1)}, u32[]{:S(2)}, u32[]{:S(2)}) async-start(f32[8,1,64]{2,1,0:T(1,128)} %get-tuple-element.79), calls=%async_computation.1 | async-start | bytes 8192 | tf_op jit(solution)/shard_map/all_to_all | solution.py:401
  91.9 10.5 %all-to-all-done.1.refs_5_ = f32[8,1,64]{2,1,0:T(1,128)S(1)} async-done(((f32[8,1,64]{2,1,0:T(1,128)}), f32[8,1,64]{2,1,0:T(1,128)S(1)}, u32[]{:S(2)}, u32[]{:S(2)}) %all-to-all-start.1) | async-done | bytes 2080 | tf_op jit(solution)/shard_map/all_to_all | solution.py:401
  102.5 2.0 %find_coefs.1 = (f32[128,1]{1,0:T(8,128)S(1)}, bf16[512,2688]{1,0:T(8,128)(2,1)S(1)}) custom-call(s32[2]{0:T(128)S(1)} %pad_add_fusion.refs_0_.place_ref, f32[8,128]{1,0:T(8,128)S(1)} %pad_maximum_fusion.refs_1_.refs_0_, bf16[128,2560]{1,0:T(8,128)(2,1)S(1)} %bitcast.94, ...), custom_call_target="tpu_custom_call", output_to_operand_aliasing={{1}: (6, {})} | custom-call | bytes 6177800 | tf_op jit(solution)/shard_map/find_coefs/pallas_call | solution.py:343
  104.5 1.5 copy-done
  106.6 3.9 %all-to-all-start.2 = ((bf16[8,64,2688]{2,1,0:T(8,128)(2,1)}), bf16[8,64,2688]{2,1,0:T(8,128)(2,1)S(1)}, u32[]{:S(2)}, u32[]{:S(2)}) async-start(bf16[8,64,2688]{2,1,0:T(8,128)(2,1)} %bitcast.90), calls=%async_computation.2 | async-start | bytes 5505024 | tf_op jit(solution)/shard_map/all_to_all | solution.py:401
  110.5 1.3 copy-done.12
  111.8 1.6 assemble.5
  113.4 0.9 copy-done.27
  114.3 3.4 %fusion.10 = f32[512,768]{1,0:T(8,128)} fusion(bf16[512,2560]{1,0:T(8,128)(2,1)S(1)} %assemble.5, bf16[1,1,2560,768]{3,2,1,0:T(8,128)(2,1)S(1)} %copy-done.27), kind=kOutput, calls=%fused_computation.16 | convolution fusion | flops 2013265920 | bytes 8126464 | tf_op jit(solution)/shard_map/dot_general | solution.py:526
  117.7 3.3 %fusion.4 = f32[512,768]{1,0:T(8,128)} fusion(bf16[512,2560]{1,0:T(8,128)(2,1)S(1)} %assemble.5, bf16[1,1,2560,768]{3,2,1,0:T(8,128)(2,1)S(1)} %copy-done.29), kind=kOutput, calls=%fused_computation.10 | convolution fusion | flops 2013265920 | bytes 8126464 | tf_op jit(solution)/shard_map/dot_general | solution.py:527
  121.0 1.8 assemble.4
  122.8 0.9 copy-done.25
  123.7 5.3 %multiply_convert_fusion.4 = (bf16[512,768]{1,0:T(8,128)(2,1)S(1)}, bf16[512,768]{1,0:T(8,128)(2,1)S(1)}) fusion(f32[512,768]{1,0:T(8,128)} %fusion.10, f32[512,768]{1,0:T(8,128)} %fusion.4, bf16[512,2560]{1,0:T(8,128)(2,1)S(1)} %assemble.4, bf16[1,1,768,2560]{3,2,1,0:T(8,128)(2,1)S(1)} %copy-done.25), kind=kOutput, calls=%fused_computation.24 | convolution fusion | flops 2018377728 | bytes 11272192 | tf_op jit(solution)/shard_map/dot_general | solution.py:364
  129.1 2.2 %fusion.8 = f32[512,2560]{1,0:T(8,128)S(1)} fusion(bf16[512,768]{1,0:T(8,128)(2,1)S(1)} %get-tuple-element.99, bf16[1,1,2560,768]{3,2,1,0:T(8,128)(2,1)S(1)} %copy-done.27), kind=kOutput, calls=%fused_computation.14 | convolution fusion | flops 2013265920 | bytes 9961472 | tf_op jit(solution)/shard_map/dot_general | solution.py:364
  131.8 2.3 %add_convert_fusion.refs_1_ = bf16[512,2560]{1,0:T(8,128)(2,1)S(1)} fusion(f32[512,2560]{1,0:T(8,128)S(1)} %fusion.8, bf16[512,768]{1,0:T(8,128)(2,1)S(1)} %get-tuple-element.98, bf16[1,1,2560,768]{3,2,1,0:T(8,128)(2,1)S(1)} %copy-done.30), kind=kOutput, calls=%fused_computation.1 | convolution fusion | flops 2015887360 | bytes 12582912 | tf_op jit(solution)/shard_map/dot_general | solution.py:364
  134.8 1.5 copy-done.2
  136.3 1.6 all-to-all-done.2
  137.8 4.4 %all-to-all-start.3 = ((bf16[8,64,2560]{2,1,0:T(8,128)(2,1)}), bf16[8,64,2560]{2,1,0:T(8,128)(2,1)}, u32[]{:S(2)}, u32[]{:S(2)}) async-start(bf16[8,64,2560]{2,1,0:T(8,128)(2,1)} %copy-done.2), calls=%async_computation.3 | async-start | bytes 5242880 | tf_op jit(solution)/shard_map/all_to_all | solution.py:401
  142.3 3.0 %join_forward.1 = bf16[128,2560]{1,0:T(8,128)(2,1)} custom-call(f32[8,128]{1,0:T(8,128)S(1)} %pad_maximum_fusion.refs_1_.refs_0_, bf16[512,2688]{1,0:T(8,128)(2,1)S(1)} %bitcast.87, bf16[128,2560]{1,0:T(8,128)(2,1)S(1)} %bitcast.95), custom_call_target="tpu_custom_call" | custom-call | bytes 4067328 | tf_op jit(solution)/shard_map/join_forward/pallas_call | solution.py:343
  145.2 2.2 %collective-permute-start.14 = (bf16[128,2560]{1,0:T(8,128)(2,1)}, bf16[128,2560]{1,0:T(8,128)(2,1)}, u32[]{:S(2)}, u32[]{:S(2)}) collective-permute-start(bf16[128,2560]{1,0:T(8,128)(2,1)} %join_forward.1), channel_id=1, source_target_pairs={{0,8},{8,16},{16,24},{24,32},{32,40},{40,48},{48,56},{56,64},{64,7... | collective-permute-start | bytes 1966088 | tf_op jit(solution)/shard_map/ppermute | solution.py:26
  148.3 6.3 %convolution_convert_fusion.1 = bf16[2560,768]{1,0:T(8,128)(2,1)} fusion(bf16[512,2560]{1,0:T(8,128)(2,1)} %copy-done.5, bf16[512,768]{1,0:T(8,128)(2,1)} %copy-done.31, f32[512]{0:T(512)S(1)} %select_n.61), kind=kOutput, calls=%fused_computation.3 | convolution fusion | flops 2016411648 | bytes 7342080 | tf_op jit(solution)/shard_map/dot_general | solution.py:358
  154.7 4.2 %convolution_convert_fusion = bf16[2560,768]{1,0:T(8,128)(2,1)} fusion(bf16[512,2560]{1,0:T(8,128)(2,1)S(1)} %copy-done.6, bf16[512,768]{1,0:T(8,128)(2,1)S(1)} %copy-done.35, f32[512]{0:T(512)S(1)} %select_n.61), kind=kOutput, calls=%fused_computation.2 | convolution fusion | flops 2016411648 | bytes 7342080 | tf_op jit(solution)/shard_map/dot_general | solution.py:358
  159.0 4.4 %convolution_convert_fusion.2 = bf16[768,2560]{1,0:T(8,128)(2,1)} fusion(bf16[512,2560]{1,0:T(8,128)(2,1)S(1)} %copy-done.8, f32[512,768]{1,0:T(8,128)S(1)} %copy-done.33, f32[512]{0:T(512)S(1)} %select_n.61, f32[512,768]{1,0:T(8,128)S(1)} %copy-done.32), kind=kOutput, calls=%fused_computation.4 | convolution fusion | flops 2018770944 | bytes 9701376 | tf_op jit(solution)/shard_map/dot_general | solution.py:358
  163.3 11.2 %all-to-all-done.3 = bf16[8,64,2560]{2,1,0:T(8,128)(2,1)} async-done(((bf16[8,64,2560]{2,1,0:T(8,128)(2,1)}), bf16[8,64,2560]{2,1,0:T(8,128)(2,1)}, u32[]{:S(2)}, u32[]{:S(2)}) %all-to-all-start.3) | async-done | bytes 2621472 | tf_op jit(solution)/shard_map/all_to_all | solution.py:401
  174.6 3.3 %join_backward.1 = (bf16[128,2560]{1,0:T(8,128)(2,1)S(1)}, f32[1,2560]{1,0:T(1,128)S(1)}) custom-call(s32[2]{0:T(128)S(1)} %pad_add_fusion.refs_0_.place_ref, f32[8,128]{1,0:T(8,128)S(1)} %pad_maximum_fusion.refs_1_.refs_0_, bf16[512,2560]{1,0:T(8,128)(2,1)} %bitcast.20.refs_2_, bf16[128,2560]{1,0:T(8,128)(2,1)S(1)} %copy-done.4, ...), custom_call_target="tpu_custom_call" | custom-call | bytes 4622856 | tf_op jit(solution)/shard_map/join_backward/pallas_call | solution.py:343
  177.9 1.9 collective-permute-start.15
  179.8 0.9 collective-permute-start.16
  180.7 4.3 %collective-permute-done.16 = f32[1,2560]{1,0:T(1,128)S(1)} collective-permute-done((f32[1,2560]{1,0:T(1,128)S(1)}, f32[1,2560]{1,0:T(1,128)S(1)}, u32[]{:S(2)}, u32[]{:S(2)}) %collective-permute-start.16) | collective-permute-done | bytes 10272 | tf_op jit(solution)/shard_map/ppermute | solution.py:579
  185.1 3.7 %collective-permute-done.17 = f32[1,2560]{1,0:T(1,128)S(1)} collective-permute-done((f32[1,2560]{1,0:T(1,128)S(1)}, f32[1,2560]{1,0:T(1,128)S(1)}, u32[]{:S(2)}, u32[]{:S(2)}) %collective-permute-start.17) | collective-permute-done | bytes 10272 | tf_op jit(solution)/shard_map/ppermute | solution.py:579
  188.9 2.0 %copy_rows.1 = bf16[128,2560]{1,0:T(8,128)(2,1)} custom-call(bf16[128,2560]{1,0:T(8,128)(2,1)} %collective-permute-done.14.in_ref, f32[1,2560]{1,0:T(1,128)S(1)} %get-tuple-element.93.unused_ref), custom_call_target="tpu_custom_call" | custom-call | bytes 1320960 | tf_op jit(solution)/shard_map/copy_rows/pallas_call | solution.py:343
  190.9 1.7 collective-permute-done.18
  193.2 0.8 copy.23
  (103 shorter events, 10.2 us)
Async XLA Ops:
  0.6 31.2 %copy-start.1 = (bf16[1,128,2560]{2,1,0:T(8,128)(2,1)S(1)}, bf16[1,128,2560]{2,1,0:T(8,128)(2,1)}, u32[]{:S(2)}) copy-start(bf16[1,128,2560]{2,1,0:T(8,128)(2,1)} %param.13) | copy-start | bytes 1966084
  0.6 31.2 %copy-start.17 = (f32[1,2560]{1,0:T(1,128)S(1)}, f32[1,2560]{1,0:T(1,128)}, u32[]{:S(2)}) copy-start(f32[1,2560]{1,0:T(1,128)} %refs_6_.1) | copy-start | bytes 30724
  0.7 19.1 %collective-permute-start = (bf16[128,2560]{1,0:T(8,128)(2,1)}, bf16[128,2560]{1,0:T(8,128)(2,1)S(1)}, u32[]{:S(2)}, u32[]{:S(2)}) collective-permute-start(bf16[128,2560]{1,0:T(8,128)(2,1)} %bitcast.91), channel_id=1, source_target_pairs={{0,2},{1,3},{2,4},{3,5},{4,6},{5,7},{6,0},{7,1},{8,10},{9,11},{10,... | collective-permute-start | bytes 1966088 | tf_op jit(solution)/shard_map/ppermute | solution.py:404
  2.6 17.1 %collective-permute-start.1 = (bf16[128,2560]{1,0:T(8,128)(2,1)}, bf16[128,2560]{1,0:T(8,128)(2,1)S(1)}, u32[]{:S(2)}, u32[]{:S(2)}) collective-permute-start(bf16[128,2560]{1,0:T(8,128)(2,1)} %bitcast.92), channel_id=1, source_target_pairs={{0,6},{1,7},{2,0},{3,1},{4,2},{5,3},{6,4},{7,5},{8,14},{9,15},{10,... | collective-permute-start | bytes 1966088 | tf_op jit(solution)/shard_map/ppermute | solution.py:404
  4.8 16.6 %collective-permute-start.2 = (bf16[128,2560]{1,0:T(8,128)(2,1)}, bf16[128,2560]{1,0:T(8,128)(2,1)S(1)}, u32[]{:S(2)}, u32[]{:S(2)}) collective-permute-start(bf16[128,2560]{1,0:T(8,128)(2,1)} %bitcast.96), channel_id=1, source_target_pairs={{0,1},{1,0},{2,3},{3,2},{4,5},{5,4},{6,7},{7,6},{8,9},{9,8},{10,11... | collective-permute-start | bytes 1966088 | tf_op jit(solution)/shard_map/ppermute | solution.py:404
  9.1 18.5 %all-to-all-start = ((f32[8,8,128]{2,1,0:T(8,128)}), f32[8,8,128]{2,1,0:T(8,128)S(1)}, u32[]{:S(2)}, u32[]{:S(2)}) async-start(f32[8,8,128]{2,1,0:T(8,128)} %broadcast_in_dim.37), calls=%async_computation | async-start | bytes 65536 | tf_op jit(solution)/shard_map/all_to_all | solution.py:401
  21.4 1.5 copy-start.20
  22.2 21.1 %copy-start.22 = (f32[2560]{0:T(1024)S(1)}, f32[2560]{0:T(1024)}, u32[]{:S(2)}) copy-start(f32[2560]{0:T(1024)} %param.24) | copy-start | bytes 30724
  22.2 21.2 %copy-start.13 = (bf16[1,128,2560]{2,1,0:T(8,128)(2,1)S(1)}, bf16[1,128,2560]{2,1,0:T(8,128)(2,1)}, u32[]{:S(2)}) copy-start(bf16[1,128,2560]{2,1,0:T(8,128)(2,1)} %param.15) | copy-start | bytes 1966084
  22.2 9.6 %collective-permute-start.3 = (bf16[64,2560]{1,0:T(8,128)(2,1)}, bf16[64,2560]{1,0:T(8,128)(2,1)}, u32[]{:S(2)}, u32[]{:S(2)}) collective-permute-start(bf16[64,2560]{1,0:T(8,128)(2,1)} %slice.15), channel_id=1, source_target_pairs={{0,2},{1,3},{2,4},{3,5},{4,6},{5,7},{6,0},{7,1},{8,10},{9,11},{10,... | collective-permute-start | bytes 983048 | tf_op jit(solution)/shard_map/ppermute | solution.py:404
  23.0 8.9 %collective-permute-start.4 = (bf16[64,2560]{1,0:T(8,128)(2,1)}, bf16[64,2560]{1,0:T(8,128)(2,1)}, u32[]{:S(2)}, u32[]{:S(2)}) collective-permute-start(bf16[64,2560]{1,0:T(8,128)(2,1)} %slice.16), channel_id=1, source_target_pairs={{0,6},{1,7},{2,0},{3,1},{4,2},{5,3},{6,4},{7,5},{8,14},{9,15},{10,... | collective-permute-start | bytes 983048 | tf_op jit(solution)/shard_map/ppermute | solution.py:404
  27.6 37.6 %copy-start.3 = (bf16[128,2560]{1,0:T(8,128)(2,1)}, bf16[128,2560]{1,0:T(8,128)(2,1)S(1)}, u32[]{:S(2)}) copy-start(bf16[128,2560]{1,0:T(8,128)(2,1)S(1)} %bitcast_select_fusion.own_ref.refs_3_) | copy-start | bytes 1966084
  27.7 15.7 %copy-start.21 = (bf16[128,2560]{1,0:T(8,128)(2,1)S(1)}, bf16[128,2560]{1,0:T(8,128)(2,1)}, u32[]{:S(2)}) copy-start(bf16[128,2560]{1,0:T(8,128)(2,1)} %copy-done.20) | copy-start | bytes 1966084
  37.1 1.1 copy-start.9
  38.2 38.6 %collective-permute-start.13 = (bf16[256,2560]{1,0:T(8,128)(2,1)}, bf16[256,2560]{1,0:T(8,128)(2,1)}, u32[]{:S(2)}, u32[]{:S(2)}) collective-permute-start(bf16[256,2560]{1,0:T(8,128)(2,1)} %get-tuple-element.78), channel_id=1, source_target_pairs={{0,1},{1,0},{2,3},{3,2},{4,5},{5,4},{6,7},{7,6},{8,9},{9,8},{10,11... | collective-permute-start | bytes 3932168 | tf_op jit(solution)/shard_map/ppermute | solution.py:404
  39.7 15.6 %collective-permute-start.5 = (bf16[128,2560]{1,0:T(8,128)(2,1)S(1)}, bf16[128,2560]{1,0:T(8,128)(2,1)S(1)}, u32[]{:S(2)}, u32[]{:S(2)}) collective-permute-start(bf16[128,2560]{1,0:T(8,128)(2,1)S(1)} %bitcast_select_fusion.own_ref.refs_3_), channel_id=1, source_target_pairs={{0,2},{1,3},{2,4},{3,5},{4,6},{5,7},{6,0},{7,1},{8,10},{9,11},{10,... | collective-permute-start | bytes 1966088 | tf_op jit(solution)/shard_map/ppermute | solution.py:404
  40.4 14.8 %collective-permute-start.6 = (bf16[128,2560]{1,0:T(8,128)(2,1)S(1)}, bf16[128,2560]{1,0:T(8,128)(2,1)S(1)}, u32[]{:S(2)}, u32[]{:S(2)}) collective-permute-start(bf16[128,2560]{1,0:T(8,128)(2,1)S(1)} %bitcast_select_fusion.own_ref.refs_3_), channel_id=1, source_target_pairs={{0,6},{1,7},{2,0},{3,1},{4,2},{5,3},{6,4},{7,5},{8,14},{9,15},{10,... | collective-permute-start | bytes 1966088 | tf_op jit(solution)/shard_map/ppermute | solution.py:404
  48.6 0.8 copy-start.15
  56.0 8.5 %collective-permute-start.7 = (bf16[64,2560]{1,0:T(8,128)(2,1)}, bf16[64,2560]{1,0:T(8,128)(2,1)S(1)}, u32[]{:S(2)}, u32[]{:S(2)}) collective-permute-start(bf16[64,2560]{1,0:T(8,128)(2,1)} %slice.17), channel_id=1, source_target_pairs={{0,2},{1,3},{2,4},{3,5},{4,6},{5,7},{6,0},{7,1},{8,10},{9,11},{10,... | collective-permute-start | bytes 983048 | tf_op jit(solution)/shard_map/ppermute | solution.py:404
  57.9 7.3 %collective-permute-start.8 = (bf16[64,2560]{1,0:T(8,128)(2,1)}, bf16[64,2560]{1,0:T(8,128)(2,1)S(1)}, u32[]{:S(2)}, u32[]{:S(2)}) collective-permute-start(bf16[64,2560]{1,0:T(8,128)(2,1)} %slice.18), channel_id=1, source_target_pairs={{0,6},{1,7},{2,0},{3,1},{4,2},{5,3},{6,4},{7,5},{8,14},{9,15},{10,... | collective-permute-start | bytes 983048 | tf_op jit(solution)/shard_map/ppermute | solution.py:404
  60.1 16.7 %copy-start.10 = (bf16[256,2560]{1,0:T(8,128)(2,1)S(1)}, bf16[256,2560]{1,0:T(8,128)(2,1)}, u32[]{:S(2)}) copy-start(bf16[256,2560]{1,0:T(8,128)(2,1)} %copy-done.9) | copy-start | bytes 3932164
  69.9 1.1 copy-start.11
  70.9 35.7 %collective-permute-start.9 = (bf16[128,2560]{1,0:T(8,128)(2,1)}, bf16[128,2560]{1,0:T(8,128)(2,1)}, u32[]{:S(2)}, u32[]{:S(2)}) collective-permute-start(bf16[128,2560]{1,0:T(8,128)(2,1)} %get-tuple-element.69), channel_id=1, source_target_pairs={{0,2},{1,3},{2,4},{3,5},{4,6},{5,7},{6,0},{7,1},{8,10},{9,11},{10,... | collective-permute-start | bytes 1966088 | tf_op jit(solution)/shard_map/ppermute | solution.py:404
  72.7 33.9 %collective-permute-start.10 = (bf16[128,2560]{1,0:T(8,128)(2,1)}, bf16[128,2560]{1,0:T(8,128)(2,1)}, u32[]{:S(2)}, u32[]{:S(2)}) collective-permute-start(bf16[128,2560]{1,0:T(8,128)(2,1)} %get-tuple-element.70), channel_id=1, source_target_pairs={{0,6},{1,7},{2,0},{3,1},{4,2},{5,3},{6,4},{7,5},{8,14},{9,15},{10,... | collective-permute-start | bytes 1966088 | tf_op jit(solution)/shard_map/ppermute | solution.py:404
  74.2 32.4 %collective-permute-start.11 = (bf16[128,2560]{1,0:T(8,128)(2,1)}, bf16[128,2560]{1,0:T(8,128)(2,1)}, u32[]{:S(2)}, u32[]{:S(2)}) collective-permute-start(bf16[128,2560]{1,0:T(8,128)(2,1)} %get-tuple-element.71), channel_id=1, source_target_pairs={{0,4},{1,5},{2,6},{3,7},{4,0},{5,1},{6,2},{7,3},{8,12},{9,13},{10,... | collective-permute-start | bytes 1966088 | tf_op jit(solution)/shard_map/ppermute | solution.py:404
  76.2 30.4 %collective-permute-start.12 = (bf16[256,2560]{1,0:T(8,128)(2,1)}, bf16[256,2560]{1,0:T(8,128)(2,1)}, u32[]{:S(2)}, u32[]{:S(2)}) collective-permute-start(bf16[256,2560]{1,0:T(8,128)(2,1)} %get-tuple-element.72), channel_id=1, source_target_pairs={{0,1},{1,0},{2,3},{3,2},{4,5},{5,4},{6,7},{7,6},{8,9},{9,8},{10,11... | collective-permute-start | bytes 3932168 | tf_op jit(solution)/shard_map/ppermute | solution.py:404
  76.8 2.5 %copy-start.26 = (bf16[1,1,2560,768]{3,2,1,0:T(8,128)(2,1)S(1)}, bf16[1,1,2560,768]{3,2,1,0:T(8,128)(2,1)}, u32[]{:S(2)}) copy-start(bf16[1,1,2560,768]{3,2,1,0:T(8,128)(2,1)} %param.20) | copy-start | bytes 11796484
  79.3 2.2 %copy-start.28 = (bf16[1,1,2560,768]{3,2,1,0:T(8,128)(2,1)S(1)}, bf16[1,1,2560,768]{3,2,1,0:T(8,128)(2,1)}, u32[]{:S(2)}) copy-start(bf16[1,1,2560,768]{3,2,1,0:T(8,128)(2,1)} %param.21) | copy-start | bytes 11796484
  81.5 2.3 %copy-start.24 = (bf16[1,1,768,2560]{3,2,1,0:T(8,128)(2,1)S(1)}, bf16[1,1,768,2560]{3,2,1,0:T(8,128)(2,1)}, u32[]{:S(2)}) copy-start(bf16[1,1,768,2560]{3,2,1,0:T(8,128)(2,1)} %param.22) | copy-start | bytes 11796484
  86.0 5.7 %copy-start.23 = (s32[128]{0:T(128)S(1)}, s32[128]{0:T(128)}, u32[]{:S(2)}) copy-start(s32[128]{0:T(128)} %param.25) | copy-start | bytes 1540
  88.0 14.5 %all-to-all-start.1 = ((f32[8,1,64]{2,1,0:T(1,128)}), f32[8,1,64]{2,1,0:T(1,128)S(1)}, u32[]{:S(2)}, u32[]{:S(2)}) async-start(f32[8,1,64]{2,1,0:T(1,128)} %get-tuple-element.79), calls=%async_computation.1 | async-start | bytes 8192 | tf_op jit(solution)/shard_map/all_to_all | solution.py:401
  104.4 1.5 copy-start
  106.0 0.6 copy-start.18
  106.6 31.2 %all-to-all-start.2 = ((bf16[8,64,2688]{2,1,0:T(8,128)(2,1)}), bf16[8,64,2688]{2,1,0:T(8,128)(2,1)S(1)}, u32[]{:S(2)}, u32[]{:S(2)}) async-start(bf16[8,64,2688]{2,1,0:T(8,128)(2,1)} %bitcast.90), calls=%async_computation.2 | async-start | bytes 5505024 | tf_op jit(solution)/shard_map/all_to_all | solution.py:401
  110.5 1.3 copy-start.12
  111.8 2.5 %copy-start.27 = (bf16[1,1,2560,768]{3,2,1,0:T(8,128)(2,1)S(1)}, bf16[1,1,2560,768]{3,2,1,0:T(8,128)(2,1)}, u32[]{:S(2)}) copy-start(bf16[1,1,2560,768]{3,2,1,0:T(8,128)(2,1)} %param.20) | copy-start | bytes 11796484
  114.3 3.4 %copy-start.5 = (bf16[512,2560]{1,0:T(8,128)(2,1)}, bf16[512,2560]{1,0:T(8,128)(2,1)S(1)}, u32[]{:S(2)}) copy-start(bf16[512,2560]{1,0:T(8,128)(2,1)S(1)} %assemble.5) | copy-start | bytes 7864324
  114.3 3.4 %copy-start.29 = (bf16[1,1,2560,768]{3,2,1,0:T(8,128)(2,1)S(1)}, bf16[1,1,2560,768]{3,2,1,0:T(8,128)(2,1)}, u32[]{:S(2)}) copy-start(bf16[1,1,2560,768]{3,2,1,0:T(8,128)(2,1)} %param.21) | copy-start | bytes 11796484
  117.7 3.3 %copy-start.16 = (bf16[128,2560]{1,0:T(8,128)(2,1)S(1)}, bf16[128,2560]{1,0:T(8,128)(2,1)}, u32[]{:S(2)}) copy-start(bf16[128,2560]{1,0:T(8,128)(2,1)} %copy-done.15) | copy-start | bytes 1966084
  121.0 2.7 %copy-start.25 = (bf16[1,1,768,2560]{3,2,1,0:T(8,128)(2,1)S(1)}, bf16[1,1,768,2560]{3,2,1,0:T(8,128)(2,1)}, u32[]{:S(2)}) copy-start(bf16[1,1,768,2560]{3,2,1,0:T(8,128)(2,1)} %param.22) | copy-start | bytes 11796484
  123.7 5.4 %copy-start.7 = (bf16[512,2560]{1,0:T(8,128)(2,1)}, bf16[512,2560]{1,0:T(8,128)(2,1)S(1)}, u32[]{:S(2)}) copy-start(bf16[512,2560]{1,0:T(8,128)(2,1)S(1)} %assemble.4) | copy-start | bytes 7864324
  129.1 2.3 %copy-start.31 = (bf16[512,768]{1,0:T(8,128)(2,1)}, bf16[512,768]{1,0:T(8,128)(2,1)S(1)}, u32[]{:S(2)}) copy-start(bf16[512,768]{1,0:T(8,128)(2,1)S(1)} %get-tuple-element.99) | copy-start | bytes 2359300
  129.1 2.3 %copy-start.34 = (bf16[512,768]{1,0:T(8,128)(2,1)}, bf16[512,768]{1,0:T(8,128)(2,1)S(1)}, u32[]{:S(2)}) copy-start(bf16[512,768]{1,0:T(8,128)(2,1)S(1)} %get-tuple-element.98) | copy-start | bytes 2359300
  129.1 2.7 %copy-start.30 = (bf16[1,1,2560,768]{3,2,1,0:T(8,128)(2,1)S(1)}, bf16[1,1,2560,768]{3,2,1,0:T(8,128)(2,1)}, u32[]{:S(2)}) copy-start(bf16[1,1,2560,768]{3,2,1,0:T(8,128)(2,1)} %param.21) | copy-start | bytes 11796484
  134.8 1.5 copy-start.2
  137.8 36.7 %all-to-all-start.3 = ((bf16[8,64,2560]{2,1,0:T(8,128)(2,1)}), bf16[8,64,2560]{2,1,0:T(8,128)(2,1)}, u32[]{:S(2)}, u32[]{:S(2)}) async-start(bf16[8,64,2560]{2,1,0:T(8,128)(2,1)} %copy-done.2), calls=%async_computation.3 | async-start | bytes 5242880 | tf_op jit(solution)/shard_map/all_to_all | solution.py:401
  145.2 43.7 %collective-permute-start.14 = (bf16[128,2560]{1,0:T(8,128)(2,1)}, bf16[128,2560]{1,0:T(8,128)(2,1)}, u32[]{:S(2)}, u32[]{:S(2)}) collective-permute-start(bf16[128,2560]{1,0:T(8,128)(2,1)} %join_forward.1), channel_id=1, source_target_pairs={{0,8},{8,16},{16,24},{24,32},{32,40},{40,48},{48,56},{56,64},{64,7... | collective-permute-start | bytes 1966088 | tf_op jit(solution)/shard_map/ppermute | solution.py:26
  148.3 6.3 %copy-start.6 = (bf16[512,2560]{1,0:T(8,128)(2,1)S(1)}, bf16[512,2560]{1,0:T(8,128)(2,1)}, u32[]{:S(2)}) copy-start(bf16[512,2560]{1,0:T(8,128)(2,1)} %copy-done.5) | copy-start | bytes 7864324
  148.3 6.3 %copy-start.35 = (bf16[512,768]{1,0:T(8,128)(2,1)S(1)}, bf16[512,768]{1,0:T(8,128)(2,1)}, u32[]{:S(2)}) copy-start(bf16[512,768]{1,0:T(8,128)(2,1)} %copy-done.34) | copy-start | bytes 2359300
  154.7 4.3 %copy-start.8 = (bf16[512,2560]{1,0:T(8,128)(2,1)S(1)}, bf16[512,2560]{1,0:T(8,128)(2,1)}, u32[]{:S(2)}) copy-start(bf16[512,2560]{1,0:T(8,128)(2,1)} %copy-done.7) | copy-start | bytes 7864324
  154.7 4.3 %copy-start.32 = (f32[512,768]{1,0:T(8,128)S(1)}, f32[512,768]{1,0:T(8,128)}, u32[]{:S(2)}) copy-start(f32[512,768]{1,0:T(8,128)} %fusion.10) | copy-start | bytes 4718596
  154.7 4.3 %copy-start.33 = (f32[512,768]{1,0:T(8,128)S(1)}, f32[512,768]{1,0:T(8,128)}, u32[]{:S(2)}) copy-start(f32[512,768]{1,0:T(8,128)} %fusion.4) | copy-start | bytes 4718596
  158.9 15.6 %copy-start.4 = (bf16[128,2560]{1,0:T(8,128)(2,1)S(1)}, bf16[128,2560]{1,0:T(8,128)(2,1)}, u32[]{:S(2)}) copy-start(bf16[128,2560]{1,0:T(8,128)(2,1)} %copy-done.3) | copy-start | bytes 1966084
  158.9 15.6 %copy-start.14 = (bf16[1,128,2560]{2,1,0:T(8,128)(2,1)S(1)}, bf16[1,128,2560]{2,1,0:T(8,128)(2,1)}, u32[]{:S(2)}) copy-start(bf16[1,128,2560]{2,1,0:T(8,128)(2,1)} %param.15) | copy-start | bytes 1966084
  158.9 15.6 %copy-start.19 = (f32[128,1]{1,0:T(8,128)S(1)}, f32[128,1]{1,0:T(8,128)}, u32[]{:S(2)}) copy-start(f32[128,1]{1,0:T(8,128)} %copy-done.18) | copy-start | bytes 1540
  177.9 15.3 %collective-permute-start.15 = (bf16[128,2560]{1,0:T(8,128)(2,1)S(1)}, bf16[128,2560]{1,0:T(8,128)(2,1)S(1)}, u32[]{:S(2)}, u32[]{:S(2)}) collective-permute-start(bf16[128,2560]{1,0:T(8,128)(2,1)S(1)} %get-tuple-element.94), channel_id=1, source_target_pairs={{8,0},{16,8},{24,16},{32,24},{40,32},{48,40},{56,48},{64,56},{72,6... | collective-permute-start | bytes 1966088 | tf_op jit(solution)/shard_map/ppermute | solution.py:26
  179.8 5.3 %collective-permute-start.16 = (f32[1,2560]{1,0:T(1,128)S(1)}, f32[1,2560]{1,0:T(1,128)S(1)}, u32[]{:S(2)}, u32[]{:S(2)}) collective-permute-start(f32[1,2560]{1,0:T(1,128)S(1)} %get-tuple-element.93.unused_ref), channel_id=1, source_target_pairs={{0,4},{1,5},{2,6},{3,7},{4,0},{5,1},{6,2},{7,3},{8,12},{9,13},{10,... | collective-permute-start | bytes 30728 | tf_op jit(solution)/shard_map/ppermute | solution.py:579
  185.1 3.8 %collective-permute-start.17 = (f32[1,2560]{1,0:T(1,128)S(1)}, f32[1,2560]{1,0:T(1,128)S(1)}, u32[]{:S(2)}, u32[]{:S(2)}) collective-permute-start(f32[1,2560]{1,0:T(1,128)S(1)} %add.63), channel_id=1, source_target_pairs={{0,2},{1,3},{2,0},{3,1},{4,6},{5,7},{6,4},{7,5},{8,10},{9,11},{10,... | collective-permute-start | bytes 30728 | tf_op jit(solution)/shard_map/ppermute | solution.py:579
  188.8 3.8 %collective-permute-start.18 = (f32[1,2560]{1,0:T(1,128)S(1)}, f32[1,2560]{1,0:T(1,128)S(1)}, u32[]{:S(2)}, u32[]{:S(2)}) collective-permute-start(f32[1,2560]{1,0:T(1,128)S(1)} %add.64), channel_id=1, source_target_pairs={{0,1},{1,0},{2,3},{3,2},{4,5},{5,4},{6,7},{7,6},{8,9},{9,8},{10,11... | collective-permute-start | bytes 30728 | tf_op jit(solution)/shard_map/ppermute | solution.py:579
